TPU v7x, 32 devices: a whole 2x2x4 slice. The times are simulated.
32 devices in a mesh: vox: 4 (over x, core), mem: 8 (over z, y).
Axes of the slice: x: 2, y: 2, z: 4, core: 2. Of those that a mesh axis runs over, the one named last changes fastest.
Arguments:
- ensemble: bfloat16 [256, 65536], P('mem', 'vox'), may hold values from -6 to 6
- partials: float32 [4, 256, 16384], P('vox', 'mem'), may hold values from -6 to 6
- perturb: float32 [256, 16384], P('mem', 'vox'), may hold values from -6 to 6
- observed: float32 [16384], P('vox'), may hold values from -6 to 6
- variance: float32 [16384], P('vox'), may hold values from 0.5 to 2
- obs_lists: int32 [512, 16], P(('vox', 'mem')), may hold values from 0 to 31, all different within a row
- taper_index: int32 [512, 16], P(('vox', 'mem')), may hold values from 0 to 15
- taper_table: float32 [16], replicated, may hold values from 0.1 to 1
Outputs:
- updated: bfloat16 [256, 65536], P('mem', 'vox')
All inputs are finite; a program needn't handle non-finite values.
Results may differ from a plain program's by a relative error of at most 0.017.
Values may be sent and summed in bfloat16 or wider, within the bound.
No kernel may reach another device: no remote copies, remote signals or barrier semaphores. Data moves between devices by JAX's collectives and lax.ppermute only.
A program may use at most 128 MiB of HBM per device.

v0:
```python
import jax
import jax.numpy as jnp
from jax import lax
from jax.sharding import PartitionSpec as P

OB = 128


def center(values):
    as_float = values.astype(jnp.float32)
    return (as_float - jnp.mean(as_float, axis=0, keepdims=True)).astype(jnp.bfloat16)


def block_moments(obs_anom, weights):
    return jnp.einsum("kbi,lbi->bkl", obs_anom, weights, preferred_element_type=jnp.float32)


def from_moments(moments, coeff, state_anom):
    high = lax.Precision.HIGHEST
    combined = jnp.einsum("bo,okl->bkl", coeff, moments, precision=high).astype(jnp.bfloat16)
    return jnp.einsum("kbc,bkl->lbc", state_anom, combined, preferred_element_type=jnp.float32)


def local(ensemble, partials, perturb, observed, variance, obs_lists, taper_index, taper_table):
    summed = lax.psum_scatter(
        partials[0].astype(jnp.bfloat16), "vox", scatter_dimension=1, tiled=True
    )
    weights = (
        (observed[None, :] + perturb - summed.astype(jnp.float32)) / variance[None, :]
    ).astype(jnp.bfloat16)
    members = lax.all_to_all(ensemble, "mem", split_axis=1, concat_axis=0, tiled=True)
    count = members.shape[0]
    blocks = obs_lists.shape[0]
    cells = members.shape[1] // blocks
    groups = weights.shape[1] // OB
    state_anom = center(members).reshape(count, blocks, cells)
    table_hits = (
        taper_index[:, :, None] == jnp.arange(taper_table.shape[0], dtype=jnp.int32)[None, None, :]
    ).astype(jnp.float32)
    tapers = jnp.sum(table_hits * taper_table[None, None, :], axis=2)
    picks = (obs_lists[:, :, None] == jnp.arange(groups, dtype=jnp.int32)[None, None, :]).astype(
        jnp.float32
    )
    coeff = jnp.sum(tapers[:, :, None] * picks, axis=1)
    pred_own, wts_own = (
        lax.all_to_all(summed, "mem", split_axis=1, concat_axis=0, tiled=True),
        lax.all_to_all(weights, "mem", split_axis=1, concat_axis=0, tiled=True),
    )
    own_anom = center(pred_own).reshape(count, -1, OB)
    own_moments = block_moments(own_anom, wts_own.reshape(count, -1, OB))
    moments = lax.all_gather(own_moments.astype(jnp.bfloat16), "mem", axis=0, tiled=True).astype(
        own_moments.dtype
    )
    increment = from_moments(moments, coeff, state_anom).reshape(count, blocks * cells)
    updated = (members.astype(jnp.float32) + increment * (1.0 / (count - 1))).astype(jnp.bfloat16)
    return lax.all_to_all(updated, "mem", split_axis=0, concat_axis=1, tiled=True)


def solution(mesh):
    return jax.shard_map(
        local,
        mesh=mesh,
        in_specs=(
            P("mem", "vox"),
            P("vox", "mem", None),
            P("mem", "vox"),
            P("vox"),
            P("vox"),
            P(("vox", "mem"), None),
            P(("vox", "mem"), None),
            P(),
        ),
        out_specs=P("mem", "vox"),
        check_vma=False,
    )
```

profile of v0, /device:TPU:1, one launch (start us, length us, event | category | flops | bytes accessed | tf_op | source)
XLA Modules:
  0.0 201.5 jit_solution(8342497593390177636)
XLA Ops:
  6.5 2.7 %convert_bitcast_fusion = bf16[32,16384]{1,0:T(8,128)(2,1)} fusion(f32[1,32,16384]{2,1,0:T(8,128)} %param.9), kind=kLoop, calls=%fused_computation.13 | loop fusion | flops 524288 | bytes 3145728 | tf_op jit(solution)/shard_map/convert_element_type | solution.py:26
  9.3 27.3 %reduce-scatter.2.cloned.1.call-done = bf16[32,4096]{1,0:T(8,128)(2,1)} async-done(((bf16[32,16384]{1,0:T(8,128)(2,1)}), bf16[32,4096]{1,0:T(8,128)(2,1)}) %reduce-scatter.2.cloned.1.call-update) | async-done | bytes 262160 | tf_op jit(solution)/shard_map/reduce_scatter | solution.py:25
  36.6 1.7 copy.67
  38.2 5.3 %all-to-all-start.1 = ((bf16[32,8,512]{2,0,1:T(8,128)(2,1)}), bf16[32,8,512]{2,0,1:T(8,128)(2,1)S(1)}, u32[]{:S(2)}, u32[]{:S(2)}) async-start(bf16[32,8,512]{2,0,1:T(8,128)(2,1)} %bitcast.38), calls=%async_computation.2 | async-start | bytes 524288 | tf_op jit(solution)/shard_map/all_to_all | solution.py:46
  43.5 1.0 divide_convert_fusion
  44.6 0.7 copy.66
  45.3 5.5 %all-to-all-done.1 = bf16[32,8,512]{2,0,1:T(8,128)(2,1)S(1)} async-done(((bf16[32,8,512]{2,0,1:T(8,128)(2,1)}), bf16[32,8,512]{2,0,1:T(8,128)(2,1)S(1)}, u32[]{:S(2)}, u32[]{:S(2)}) %all-to-all-start.1) | async-done | bytes 262176 | tf_op jit(solution)/shard_map/all_to_all | solution.py:46
  50.7 4.9 %all-to-all-start.2 = ((bf16[32,8,512]{2,0,1:T(8,128)(2,1)}), bf16[32,8,512]{2,0,1:T(8,128)(2,1)S(1)}, u32[]{:S(2)}, u32[]{:S(2)}) async-start(bf16[32,8,512]{2,0,1:T(8,128)(2,1)} %bitcast.37), calls=%async_computation.3 | async-start | bytes 524288 | tf_op jit(solution)/shard_map/all_to_all | solution.py:47
  55.7 0.1 convert_bitcast_fusion.1
  55.8 0.2 reshape.60
  55.9 0.1 convert_reduce_fusion.1
  56.0 6.8 %all-to-all-done.2 = bf16[32,8,512]{2,0,1:T(8,128)(2,1)S(1)} async-done(((bf16[32,8,512]{2,0,1:T(8,128)(2,1)}), bf16[32,8,512]{2,0,1:T(8,128)(2,1)S(1)}, u32[]{:S(2)}, u32[]{:S(2)}) %all-to-all-start.2) | async-done | bytes 262176 | tf_op jit(solution)/shard_map/all_to_all | solution.py:47
  62.8 0.1 reshape.59
  62.9 0.1 subtract_convert_fusion
  63.0 1.1 convolution_convert_fusion
  64.2 1.0 copy.65
  65.2 4.9 %all-to-all-start = ((bf16[32,8,2048]{2,0,1:T(8,128)(2,1)}), bf16[32,8,2048]{2,0,1:T(8,128)(2,1)S(1)}, u32[]{:S(2)}, u32[]{:S(2)}) async-start(bf16[32,8,2048]{2,0,1:T(8,128)(2,1)} %bitcast.36), calls=%async_computation | async-start | bytes 2097152 | tf_op jit(solution)/shard_map/all_to_all | solution.py:31
  70.1 0.2 select_reduce_fusion.1
  70.4 0.1 select_reduce_fusion
  70.5 40.4 %all-to-all-done = bf16[32,8,2048]{2,0,1:T(8,128)(2,1)S(1)} async-done(((bf16[32,8,2048]{2,0,1:T(8,128)(2,1)}), bf16[32,8,2048]{2,0,1:T(8,128)(2,1)S(1)}, u32[]{:S(2)}, u32[]{:S(2)}) %all-to-all-start) | async-done | bytes 1048608 | tf_op jit(solution)/shard_map/all_to_all | solution.py:31
  110.9 0.2 convert_element_type.65
  111.1 0.4 copy.47
  111.5 0.2 convert_reduce_fusion
  111.7 0.2 fusion.2
  111.9 41.0 %all-gather.2.cloned.1.call-done = bf16[32,256,256]{2,1,0:T(8,128)(2,1)} async-done(((bf16[4,256,256]{2,1,0:T(8,128)(2,1)}), bf16[32,256,256]{2,1,0:T(8,128)(2,1)}) %all-gather.2.cloned.1.call-update) | async-done | bytes 4194320 | tf_op jit(solution)/shard_map/all_gather | solution.py:51
  152.9 5.8 %fusion.6 = bf16[16,256,256]{2,0,1:T(8,128)(2,1)S(1)} fusion(bf16[32,256,256]{2,1,0:T(8,128)(2,1)} %all-gather.2.cloned.1.call-done, f32[16,32]{1,0:T(8,128)S(1)} %select_reduce_fusion), kind=kOutput, calls=%fused_computation.9 | convolution fusion | flops 403701760 | bytes 6293504 | tf_op jit(solution)/shard_map/bo,okl->bkl/dot_general | solution.py:20
  158.7 1.7 multiply_bitcast_fusion
  160.3 2.5 %copy.41 = f32[256,16,128]{2,1,0:T(8,128)} copy(f32[256,16,128]{2,0,1:T(8,128)S(1)} %multiply_bitcast_fusion) | data formatting | bytes 4194304 | tf_op jit(solution)/shard_map/mul | solution.py:55
  162.9 1.7 mul.36
  164.6 0.3 fusion.3
  164.9 28.7 %all_to_all.58 = bf16[8,32,2048]{2,1,0:T(8,128)(2,1)S(1)} all-to-all(bf16[8,32,2048]{2,1,0:T(8,128)(2,1)S(1)} %fusion.3), channel_id=1, replica_groups=mesh['vox'=4,'mem'=8] {'mem'}, dimensions={0} | all-to-all | bytes 2097152 | tf_op jit(solution)/shard_map/all_to_all | solution.py:56
  193.6 1.0 copy.46
  (20 shorter events, 0.1 us)
Async XLA Ops:
  6.5 37.0 %copy-start.1 = (f32[32,4096]{1,0:T(8,128)S(1)}, f32[32,4096]{1,0:T(8,128)}, u32[]{:S(2)}) copy-start(f32[32,4096]{1,0:T(8,128)} %param.10) | copy-start | bytes 1572868
  6.5 37.0 %copy-start.3 = (f32[4096]{0:T(1024)S(1)}, f32[4096]{0:T(1024)}, u32[]{:S(2)}) copy-start(f32[4096]{0:T(1024)} %param.11) | copy-start | bytes 49156
  6.5 37.0 %copy-start.2 = (f32[4096]{0:T(1024)S(1)}, f32[4096]{0:T(1024)}, u32[]{:S(2)}) copy-start(f32[4096]{0:T(1024)} %param.12) | copy-start | bytes 49156
  6.5 30.0 %reduce-scatter.2.cloned.1.call-start = ((), (), s32[]{:S(2)}) async-start(), calls=%async_computation.5 | async-start | bytes 1310720 | tf_op jit(solution)/shard_map/reduce_scatter | solution.py:25
  38.2 12.5 %all-to-all-start.1 = ((bf16[32,8,512]{2,0,1:T(8,128)(2,1)}), bf16[32,8,512]{2,0,1:T(8,128)(2,1)S(1)}, u32[]{:S(2)}, u32[]{:S(2)}) async-start(bf16[32,8,512]{2,0,1:T(8,128)(2,1)} %bitcast.38), calls=%async_computation.2 | async-start | bytes 524288 | tf_op jit(solution)/shard_map/all_to_all | solution.py:46
  50.7 12.1 %all-to-all-start.2 = ((bf16[32,8,512]{2,0,1:T(8,128)(2,1)}), bf16[32,8,512]{2,0,1:T(8,128)(2,1)S(1)}, u32[]{:S(2)}, u32[]{:S(2)}) async-start(bf16[32,8,512]{2,0,1:T(8,128)(2,1)} %bitcast.37), calls=%async_computation.3 | async-start | bytes 524288 | tf_op jit(solution)/shard_map/all_to_all | solution.py:47
  55.6 97.3 %all-gather.2.cloned.1.call-start = ((), (), s32[]{:S(2)}) async-start(), calls=%async_computation.6 | async-start | bytes 4718592 | tf_op jit(solution)/shard_map/all_gather | solution.py:51
  55.7 8.4 %copy-start = (bf16[32,16384]{1,0:T(8,128)(2,1)S(1)}, bf16[32,16384]{1,0:T(8,128)(2,1)}, u32[]{:S(2)}) copy-start(bf16[32,16384]{1,0:T(8,128)(2,1)} %param.8) | copy-start | bytes 3145732
  64.1 6.0 %copy-start.5 = (s32[16,16]{1,0:T(8,128)S(1)}, s32[16,16]{1,0:T(8,128)}, u32[]{:S(2)}) copy-start(s32[16,16]{1,0:T(8,128)} %param.14) | copy-start | bytes 3076
  64.2 6.0 %copy-start.6 = (f32[16]{0:T(128)S(1)}, f32[16]{0:T(128)}, u32[]{:S(2)}) copy-start(f32[16]{0:T(128)} %param.15) | copy-start | bytes 196
  64.2 6.2 %copy-start.4 = (s32[16,16]{1,0:T(8,128)S(1)}, s32[16,16]{1,0:T(8,128)}, u32[]{:S(2)}) copy-start(s32[16,16]{1,0:T(8,128)} %param.13) | copy-start | bytes 3076
  65.2 45.6 %all-to-all-start = ((bf16[32,8,2048]{2,0,1:T(8,128)(2,1)}), bf16[32,8,2048]{2,0,1:T(8,128)(2,1)S(1)}, u32[]{:S(2)}, u32[]{:S(2)}) async-start(bf16[32,8,2048]{2,0,1:T(8,128)(2,1)} %bitcast.36), calls=%async_computation | async-start | bytes 2097152 | tf_op jit(solution)/shard_map/all_to_all | solution.py:31
Sparse Core Ops, SparseCore 0:
  9.9 26.6 reduce-scatter.1
  64.3 88.5 all-gather.1
where the time goes:
time: 204 us; the launch traced here: 201 us
  waiting for transfers between devices  121 us (59%)
  blocking collectives  28.7 us (14%)
  starting transfers between devices  15.1 us (7%)
  between operations  13.6 us (7%)
  local copies, waits for them, and re-layouts  9.4 us (5%)
  matrix products  8.55 us (4%)
  other arithmetic  5.17 us (3%)
    all_gather x1, waiting for transfers between devices, local(): lax.all_gather(own_moments.astype(jnp.bfloat16), 'mem', axis=0, tiled=True)  41 us
    all_to_all x1, waiting for transfers between devices, local(): lax.all_to_all(ensemble, 'mem', split_axis=1, concat_axis=0, tiled=True)  40.4 us
    all_to_all x1, blocking collectives, local(): lax.all_to_all(updated, 'mem', split_axis=0, concat_axis=1, tiled=True)  28.7 us
    reduce_scatter x1, waiting for transfers between devices, local(): lax.psum_scatter(partials[0].astype(jnp.bfloat16), 'vox', scatter_dimensi...  27.3 us
    all_to_all x1, waiting for transfers between devices, local(): lax.all_to_all(weights, 'mem', split_axis=1, concat_axis=0, tiled=True)  6.8 us
    dot_general x1, matrix products, from_moments(): jnp.einsum('bo,okl->bkl', coeff, moments, precision=high)  5.77 us
    all_to_all x1, waiting for transfers between devices, local(): lax.all_to_all(summed, 'mem', split_axis=1, concat_axis=0, tiled=True)  5.46 us
    all_to_all x1, starting transfers between devices, local(): lax.all_to_all(summed, 'mem', split_axis=1, concat_axis=0, tiled=True)  5.25 us
  transfers between devices with their start and end apart: 5, of which 5 were waited for; matrix products, arithmetic and copies ran while one was open for 2% of the time, Pallas kernels for 0%

commit v1 on v0

v1 whole, which is shorter than its diff:
```python
import functools

import jax
import jax.numpy as jnp
from jax import lax
from jax.experimental import pallas as pl
from jax.experimental.pallas import tpu as pltpu
from jax.sharding import PartitionSpec as P

OB = 128
SUB = 8
AXES = ("vox", "mem")
BF = jnp.bfloat16
F32 = jnp.float32


class Plan:
    def __init__(self, nv, nm):
        assert nv % 2 == 0 and nm % nv == 0
        self.nv, self.nm = nv, nm
        self.half, self.inner = nv // 2, nm // nv
        self.chips = nm // 2
        self.everyone = [(v, m) for v in range(nv) for m in range(nm)]

    def device(self, v, q, h):
        x, c = divmod(v, 2)
        qx, qy = divmod(q, self.inner)
        return ((qx + x) % self.half) * 2 + h, (c * self.half + x) * self.inner + qy

    def moved(self, q, i):
        ix, iy = divmod(i, self.inner)
        return ((q // self.inner + ix) % self.half) * self.inner + (q % self.inner + iy) % self.inner

    def flat(self, pairs):
        return [(a * self.nm + b, c * self.nm + d) for (a, b), (c, d) in pairs]

    def out_to_plane(self, i):
        return self.flat([((v, m), self.device(v, self.moved(m // 2, i), m % 2)) for v, m in self.everyone])

    def back(self, i):
        return [(b, a) for a, b in self.out_to_plane(i)]

    def in_plane(self, i):
        return self.flat(
            [
                (self.device(v, q, h), self.device(v, self.moved(q, i), h))
                for v in range(self.nv)
                for q in range(self.chips)
                for h in range(2)
            ]
        )

    def core(self):
        return self.flat([((v, m), (v ^ 1, m)) for v, m in self.everyone])

    def x_shift(self, s):
        return self.flat([((v, m), ((v + 2 * s) % self.nv, m)) for v, m in self.everyone])


def cost(flops, moved):
    return pl.CostEstimate(flops=flops, bytes_accessed=moved, transcendentals=0)


def vmem(count):
    return [pl.BlockSpec(memory_space=pltpu.VMEM)] * count


def center_kernel(parts, *refs):
    out = refs[parts]
    width = out.shape[1]
    rows = refs[0].shape[0]

    def step(t, carry):
        cols = pl.ds(pl.multiple_of(t * OB, OB), OB)
        values = [r[:, cols].astype(F32) for r in refs[:parts]]
        mean = sum(jnp.sum(x, axis=0, keepdims=True) for x in values) * (1.0 / (parts * rows))
        out[:, cols] = jnp.concatenate([x - mean for x in values], axis=0).astype(BF)
        return carry

    lax.fori_loop(0, width // OB, step, 0)


def center_state(pieces):
    rows, width = pieces[0].shape
    total = rows * len(pieces)
    return pl.pallas_call(
        functools.partial(center_kernel, len(pieces)),
        out_shape=jax.ShapeDtypeStruct((total, width), BF),
        in_specs=vmem(len(pieces)),
        out_specs=vmem(1)[0],
        cost_estimate=cost(4 * total * width, 4 * total * width),
        name="center_state",
    )(*pieces)


def update_kernel(own_parts, *refs):
    n = own_parts
    own, other, pert, state = refs[:n], refs[n : 2 * n], refs[2 * n : 3 * n], refs[3 * n : 4 * n]
    obs, var, kron, anom = refs[4 * n : 4 * n + 4]
    outs = refs[4 * n + 4 : 5 * n + 4]
    stacked, combined = refs[5 * n + 4 :]
    rows = own[0].shape[0]
    count = 2 * n * rows
    lanes = n * rows
    tiles = lanes // SUB
    groups = own[0].shape[1] // OB
    blocks = combined.shape[0]

    def moment(o, carry):
        cols = pl.ds(pl.multiple_of(o * OB, OB), OB)
        mine = jnp.concatenate([r[:, cols].astype(F32) for r in own], axis=0)
        theirs = jnp.concatenate([r[:, cols].astype(F32) for r in other], axis=0)
        noise = jnp.concatenate([r[:, cols].astype(F32) for r in pert], axis=0)
        mean = (jnp.sum(mine, axis=0, keepdims=True) + jnp.sum(theirs, axis=0, keepdims=True)) * (1.0 / count)
        weights = ((obs[:, cols] + noise - mine) / var[:, cols]).astype(BF)
        anomaly = jnp.concatenate([mine - mean, theirs - mean], axis=0).astype(BF)
        m = lax.dot_general(weights, anomaly, (((1,), (1,)), ((), ())), preferred_element_type=F32)
        stacked[:, pl.ds(pl.multiple_of(o * SUB, SUB), SUB), :] = m.reshape(tiles, SUB, count)
        return carry

    lax.fori_loop(0, groups, moment, 0)

    def combine(g, carry):
        c = lax.dot_general(
            kron[...], stacked[g].astype(BF), (((1,), (0,)), ((), ())), preferred_element_type=F32
        )
        combined[:, pl.ds(pl.multiple_of(g * SUB, SUB), SUB), :] = c.reshape(blocks, SUB, count)
        return carry

    lax.fori_loop(0, tiles, combine, 0)

    cells = anom.shape[1] // blocks

    def increment(b, carry):
        cols = pl.ds(pl.multiple_of(b * cells, cells), cells)
        inc = lax.dot_general(
            combined[b].astype(BF), anom[:, cols], (((1,), (0,)), ((), ())), preferred_element_type=F32
        )
        for i in range(n):
            new = state[i][:, cols].astype(F32) + inc[i * rows : (i + 1) * rows, :] * (1.0 / (count - 1))
            outs[i][:, cols] = new.astype(BF)
        return carry

    lax.fori_loop(0, blocks, increment, 0)


def update(own, other, pert, state, obs, var, kron, anom, blocks):
    n = len(own)
    rows, data = own[0].shape
    cells = state[0].shape[1]
    count, lanes = 2 * n * rows, n * rows
    groups = data // OB
    flops = 2 * lanes * count * (data + kron.shape[0] * groups * SUB // SUB + cells)
    return pl.pallas_call(
        functools.partial(update_kernel, n),
        out_shape=[jax.ShapeDtypeStruct((rows, cells), BF)] * n,
        in_specs=vmem(4 * n + 4),
        out_specs=vmem(n),
        scratch_shapes=[
            pltpu.VMEM((lanes // SUB, groups * SUB, count), F32),
            pltpu.VMEM((blocks, lanes, count), F32),
        ],
        cost_estimate=cost(flops, 2 * (3 * lanes * data + 3 * count * cells)),
        compiler_params=pltpu.CompilerParams(vmem_limit_bytes=60 << 20),
        name="update",
    )(*own, *other, *pert, *state, obs, var, kron, anom)


def place_kernel(parts, at, *refs):
    out, sems = refs[parts], refs[parts + 1]
    width = refs[0].shape[1]
    copies = []
    for i in range(parts):
        start = pl.multiple_of(at[i] * width, OB)
        copies.append(pltpu.make_async_copy(refs[i], out.at[:, pl.ds(start, width)], sems.at[i]))
    for c in copies:
        c.start()
    for c in copies:
        c.wait()


def place(pieces, at):
    n = len(pieces)
    rows, width = pieces[0].shape
    return pl.pallas_call(
        functools.partial(place_kernel, n),
        grid_spec=pltpu.PrefetchScalarGridSpec(
            num_scalar_prefetch=1,
            in_specs=vmem(n),
            out_specs=pl.BlockSpec(memory_space=pl.ANY),
            scratch_shapes=[pltpu.SemaphoreType.DMA((n,))],
        ),
        out_shape=jax.ShapeDtypeStruct((rows, n * width), BF),
        cost_estimate=cost(0, 4 * n * rows * width),
        name="place",
    )(at, *pieces)


def local(plan, ensemble, partials, perturb, observed, variance, obs_lists, taper_index, taper_table):
    n, half = plan.chips, plan.half
    v, m = lax.axis_index("vox"), lax.axis_index("mem")
    x, core = v // 2, v % 2
    rows, data = perturb.shape
    per_chip = ensemble.shape[1] // n

    def send(value, pairs):
        return lax.ppermute(value, AXES, pairs)

    parts = partials[0].reshape(rows, half, 2, data)
    away = lax.dynamic_slice_in_dim(parts, 1 - core, 1, 2)[:, :, 0].astype(BF)
    got = send(away, plan.core())
    pair = lax.dynamic_slice_in_dim(parts, core, 1, 2)[:, :, 0] + got.astype(F32)
    total = lax.dynamic_slice_in_dim(pair, x, 1, 1)[:, 0]
    for s in range(1, half):
        piece = lax.dynamic_slice_in_dim(pair, (x + s) % half, 1, 1)[:, 0].astype(BF)
        total = total + send(piece, plan.x_shift(s)).astype(F32)
    predicted = total.astype(BF)

    groups = data // OB
    table_hits = (
        taper_index[:, :, None] == jnp.arange(taper_table.shape[0], dtype=jnp.int32)[None, None, :]
    ).astype(F32)
    tapers = jnp.sum(table_hits * taper_table[None, None, :], axis=2)
    picks = (obs_lists[:, :, None] == jnp.arange(groups, dtype=jnp.int32)[None, None, :]).astype(F32)
    coeff = jnp.sum(tapers[:, :, None] * picks, axis=1)
    own_blocks = coeff.shape[0]
    first = plan.out_to_plane(0)
    small = send(jnp.concatenate([observed, variance, coeff.reshape(-1)]), first)
    obs, var = small[:data].reshape(1, data), small[data : 2 * data].reshape(1, data)
    mine = small[2 * data :]
    theirs = send(mine, plan.core())
    coeff = jnp.where(core == 0, jnp.concatenate([mine, theirs]), jnp.concatenate([theirs, mine]))
    blocks = 2 * own_blocks
    coeff = coeff.reshape(blocks, groups)
    kron = (coeff[:, None, :, None] * jnp.eye(SUB, dtype=F32)[None, :, None, :]).astype(BF)
    kron = kron.reshape(blocks * SUB, groups * SUB)

    def chip(i):
        return plan.moved(m // 2, i)

    own_state = [
        send(lax.dynamic_slice_in_dim(ensemble, chip(i) * per_chip, per_chip, 1), plan.out_to_plane(i))
        for i in range(n)
    ]
    other_state = [send(s, plan.core()) for s in own_state]
    anom = center_state(own_state + other_state)

    noise = send(perturb.astype(BF), first)
    pert = [noise] + [send(noise, plan.in_plane(i)) for i in range(1, n)]
    arrived = send(predicted, first)
    own = [arrived] + [send(arrived, plan.in_plane(i)) for i in range(1, n)]
    other = [send(p, plan.core()) for p in own]

    new = update(own, other, pert, own_state, obs, var, kron, anom, blocks)
    back = [send(new[i], plan.back(i)) for i in range(n)]
    at = jnp.stack([chip(i) for i in range(n)]).astype(jnp.int32)
    return place(back, at)


def solution(mesh):
    plan = Plan(mesh.shape["vox"], mesh.shape["mem"])
    return jax.shard_map(
        functools.partial(local, plan),
        mesh=mesh,
        in_specs=(
            P("mem", "vox"),
            P("vox", "mem", None),
            P("mem", "vox"),
            P("vox"),
            P("vox"),
            P(("vox", "mem"), None),
            P(("vox", "mem"), None),
            P(),
        ),
        out_specs=P("mem", "vox"),
        check_vma=False,
    )
```

time: 204 us -> 154 us (0.75)
  waiting for transfers between devices: 121 us -> 41.7 us
  starting transfers between devices: 15.1 us -> 66.4 us
  blocking collectives: 28.7 us -> 0 us
  Pallas kernels: 0 us -> 26.3 us
  between operations: 13.6 us -> 0.6 us
  matrix products: 8.55 us -> 0 us
  local copies, waits for them, and re-layouts: 9.4 us -> 12.6 us
    ppermute x0 -> x28, starting transfers between devices: none -> 66.4 us  [send(): return lax.ppermute(value, AXES, pairs)]
    all_to_all x3 -> x0, waiting for transfers between devices: 52.6 us -> none  [the longest x1 40.4 us: local(): lax.all_to_all(ensemble, 'mem', split_axis=1, concat_axis=0, tiled=True)]
    ppermute x0 -> x28, waiting for transfers between devices: none -> 41.7 us  [send(): return lax.ppermute(value, AXES, pairs)]
    all_gather x1 -> x0, waiting for transfers between devices: 41 us -> none  [local(): lax.all_gather(own_moments.astype(jnp.bfloat16), 'mem', axis=0, tiled=True)]
    all_to_all x1 -> x0, blocking collectives: 28.7 us -> none  [local(): lax.all_to_all(updated, 'mem', split_axis=0, concat_axis=1, tiled=True)]
    reduce_scatter x1 -> x0, waiting for transfers between devices: 27.3 us -> none  [local(): lax.psum_scatter(partials[0].astype(jnp.bfloat16), 'vox', scatter_dimensi...]
    pallas_call x0 -> x3, Pallas kernels: none -> 26.3 us  [the longest x1 19 us: update(): pl.pallas_call(functools.partial(update_kernel, n), out_shape=[jax.ShapeD...]
    all_to_all x3 -> x0, starting transfers between devices: 15.1 us -> none  [the longest x1 5.25 us: local(): lax.all_to_all(summed, 'mem', split_axis=1, concat_axis=0, tiled=True)]
  transfers between devices with their start and end apart: 5 -> 28, of which waited for: 5 -> 8; matrix products, arithmetic and copies ran while one was open for 2% -> 8% of each run, Pallas kernels for 0% -> 3%
where the time goes in v1:
time: 154 us; the launch traced here: 153 us
  starting transfers between devices  66.4 us (43%)
  waiting for transfers between devices  41.7 us (27%)
  Pallas kernels  26.3 us (17%)
  local copies, waits for them, and re-layouts  12.6 us (8%)
  other arithmetic  5.54 us (4%)
    ppermute x28, starting transfers between devices, send(): return lax.ppermute(value, AXES, pairs)  66.4 us
    ppermute x28, waiting for transfers between devices, send(): return lax.ppermute(value, AXES, pairs)  41.7 us
    pallas_call x1, Pallas kernels, update(): pl.pallas_call(functools.partial(update_kernel, n), out_shape=[jax.ShapeD...  19 us
    pallas_call x1, Pallas kernels, center_state(): pl.pallas_call(functools.partial(center_kernel, len(pieces)), out_shape=j...  4.42 us
    convert_element_type x1, local copies, waits for them, and re-layouts, local(): (coeff[:, None, :, None] * jnp.eye(SUB, dtype=F32)[None, :, None, :]).ast...  3.49 us
  transfers between devices with their start and end apart: 28, of which 8 were waited for; matrix products, arithmetic and copies ran while one was open for 8% of the time, Pallas kernels for 3%

profile of v1, /device:TPU:1, one launch (start us, length us, event | category | flops | bytes accessed | tf_op | source)
XLA Modules:
  0.0 153.2 jit_solution(6724353861783618614)
XLA Ops:
  0.0 3.0 %reshape_squeeze.3 = f32[32,2,2,4096]{3,2,1,0:T(2,128)S(1)} reshape(f32[1,32,16384]{2,1,0:T(8,128)} %param.9) | data formatting | bytes 4194304 | tf_op jit(solution)/shard_map/reshape;squeeze | solution.py:209
  4.3 1.4 copy.18
  6.4 5.6 %collective-permute-start.10 = (bf16[32,4096]{1,0:T(8,128)(2,1)}, bf16[32,4096]{1,0:T(8,128)(2,1)S(1)}, u32[]{:S(2)}, u32[]{:S(2)}) collective-permute-start(bf16[32,4096]{1,0:T(8,128)(2,1)} %convert_element_type.47), channel_id=1, source_target_pairs={{0,0},{1,8},{2,1},{3,9},{4,16},{5,24},{6,17},{7,25},{8,4},{9,12},{... | collective-permute-start | bytes 786440 | tf_op jit(solution)/shard_map/ppermute | solution.py:207
  12.4 3.2 %collective-permute-start.18 = (f32[8704]{0:T(1024)S(1)}, f32[8704]{0:T(1024)S(1)}, u32[]{:S(2)}, u32[]{:S(2)}) collective-permute-start(f32[8704]{0:T(1024)S(1)} %pad_maximum_fusion), channel_id=1, source_target_pairs={{0,0},{1,8},{2,1},{3,9},{4,16},{5,24},{6,17},{7,25},{8,4},{9,12},{... | collective-permute-start | bytes 104456 | tf_op jit(solution)/shard_map/ppermute | solution.py:207
  17.7 1.7 %bitcast_add_fusion = f32[32,2,4096]{2,0,1:T(8,128)S(1)} fusion(f32[32,2,1,4096]{3,2,1,0:T(1,128)S(1)} %constant_dynamic-slice_fusion.5, bf16[32,2,4096]{2,0,1:T(8,128)(2,1)} %collective-permute-done), kind=kLoop, calls=%fused_computation.2 | loop fusion | flops 524288 | bytes 2621440 | tf_op jit(solution)/shard_map/add | solution.py:212
  19.5 5.4 %collective-permute-start.1 = (bf16[32,4096]{1,0:T(8,128)(2,1)S(1)}, bf16[32,4096]{1,0:T(8,128)(2,1)}, u32[]{:S(2)}, u32[]{:S(2)}) collective-permute-start(bf16[32,4096]{1,0:T(8,128)(2,1)S(1)} %fusion.2), channel_id=1, source_target_pairs={{0,16},{1,17},{2,18},{3,19},{4,20},{5,21},{6,22},{7,23},{8,24},{9,... | collective-permute-start | bytes 786440 | tf_op jit(solution)/shard_map/ppermute | solution.py:207
  25.7 4.3 %collective-permute-start.14 = (bf16[32,4096]{1,0:T(8,128)(2,1)S(1)}, bf16[32,4096]{1,0:T(8,128)(2,1)S(1)}, u32[]{:S(2)}, u32[]{:S(2)}) collective-permute-start(bf16[32,4096]{1,0:T(8,128)(2,1)S(1)} %get-tuple-element.15), channel_id=1, source_target_pairs={{0,0},{1,8},{2,1},{3,9},{4,16},{5,24},{6,17},{7,25},{8,4},{9,12},{... | collective-permute-start | bytes 786440 | tf_op jit(solution)/shard_map/ppermute | solution.py:207
  30.0 2.9 %collective-permute-start.15 = (bf16[32,4096]{1,0:T(8,128)(2,1)}, bf16[32,4096]{1,0:T(8,128)(2,1)S(1)}, u32[]{:S(2)}, u32[]{:S(2)}) collective-permute-start(bf16[32,4096]{1,0:T(8,128)(2,1)} %get-tuple-element.14), channel_id=1, source_target_pairs={{0,1},{1,9},{2,0},{3,8},{4,17},{5,25},{6,16},{7,24},{8,5},{9,13},{... | collective-permute-start | bytes 786440 | tf_op jit(solution)/shard_map/ppermute | solution.py:207
  33.0 4.9 %collective-permute-start.16 = (bf16[32,4096]{1,0:T(8,128)(2,1)S(1)}, bf16[32,4096]{1,0:T(8,128)(2,1)S(1)}, u32[]{:S(2)}, u32[]{:S(2)}) collective-permute-start(bf16[32,4096]{1,0:T(8,128)(2,1)S(1)} %get-tuple-element.16), channel_id=1, source_target_pairs={{0,16},{1,24},{2,17},{3,25},{4,0},{5,8},{6,1},{7,9},{8,20},{9,28},... | collective-permute-start | bytes 786440 | tf_op jit(solution)/shard_map/ppermute | solution.py:207
  37.9 4.1 %collective-permute-start.17 = (bf16[32,4096]{1,0:T(8,128)(2,1)S(1)}, bf16[32,4096]{1,0:T(8,128)(2,1)S(1)}, u32[]{:S(2)}, u32[]{:S(2)}) collective-permute-start(bf16[32,4096]{1,0:T(8,128)(2,1)S(1)} %get-tuple-element.13), channel_id=1, source_target_pairs={{0,17},{1,25},{2,16},{3,24},{4,1},{5,9},{6,0},{7,8},{8,21},{9,29},... | collective-permute-start | bytes 786440 | tf_op jit(solution)/shard_map/ppermute | solution.py:207
  42.0 1.7 %fusion.1 = bf16[32,4096]{1,0:T(8,128)(2,1)} fusion(bf16[32,4096]{1,0:T(8,128)(2,1)} %collective-permute-done.1, f32[32,2,4096]{2,0,1:T(8,128)S(1)} %bitcast_add_fusion, s32[]{:T(128)S(6)} %select_n.140), kind=kLoop, calls=%fused_computation.5 | loop fusion | flops 393216 | bytes 1048580 | tf_op jit(solution)/shard_map/convert_element_type | solution.py:217
  44.6 2.2 %collective-permute-start.12 = (bf16[32,4096]{1,0:T(8,128)(2,1)S(1)}, bf16[32,4096]{1,0:T(8,128)(2,1)S(1)}, u32[]{:S(2)}, u32[]{:S(2)}) collective-permute-start(bf16[32,4096]{1,0:T(8,128)(2,1)S(1)} %collective-permute-done.10.refs_8_), channel_id=1, source_target_pairs={{0,16},{8,24},{1,17},{9,25},{16,0},{24,8},{17,1},{25,9},{4,20},{12... | collective-permute-start | bytes 786440 | tf_op jit(solution)/shard_map/ppermute | solution.py:207
  46.7 16.4 %collective-permute-done.15.refs_1_.refs_13_ = bf16[32,4096]{1,0:T(8,128)(2,1)S(1)} collective-permute-done((bf16[32,4096]{1,0:T(8,128)(2,1)}, bf16[32,4096]{1,0:T(8,128)(2,1)S(1)}, u32[]{:S(2)}, u32[]{:S(2)}) %collective-permute-start.15) | collective-permute-done | bytes 262176 | tf_op jit(solution)/shard_map/ppermute | solution.py:207
  63.1 1.9 %collective-permute-start.2 = (bf16[32,4096]{1,0:T(8,128)(2,1)}, bf16[32,4096]{1,0:T(8,128)(2,1)}, u32[]{:S(2)}, u32[]{:S(2)}) collective-permute-start(bf16[32,4096]{1,0:T(8,128)(2,1)} %fusion.1), channel_id=1, source_target_pairs={{0,0},{1,8},{2,1},{3,9},{4,16},{5,24},{6,17},{7,25},{8,4},{9,12},{... | collective-permute-start | bytes 786440 | tf_op jit(solution)/shard_map/ppermute | solution.py:207
  65.1 1.8 %collective-permute-start.20 = (bf16[32,4096]{1,0:T(8,128)(2,1)S(1)}, bf16[32,4096]{1,0:T(8,128)(2,1)S(1)}, u32[]{:S(2)}, u32[]{:S(2)}) collective-permute-start(bf16[32,4096]{1,0:T(8,128)(2,1)S(1)} %collective-permute-done.14.refs_0_.refs_12_), channel_id=1, source_target_pairs={{0,8},{1,9},{2,10},{3,11},{4,12},{5,13},{6,14},{7,15},{8,0},{9,1},... | collective-permute-start | bytes 786440 | tf_op jit(solution)/shard_map/ppermute | solution.py:207
  67.6 3.5 %collective-permute-done.2.refs_0_ = bf16[32,4096]{1,0:T(8,128)(2,1)} collective-permute-done((bf16[32,4096]{1,0:T(8,128)(2,1)}, bf16[32,4096]{1,0:T(8,128)(2,1)}, u32[]{:S(2)}, u32[]{:S(2)}) %collective-permute-start.2) | collective-permute-done | bytes 262176 | tf_op jit(solution)/shard_map/ppermute | solution.py:207
  71.1 4.7 %collective-permute-start.3 = (bf16[32,4096]{1,0:T(8,128)(2,1)}, bf16[32,4096]{1,0:T(8,128)(2,1)}, u32[]{:S(2)}, u32[]{:S(2)}) collective-permute-start(bf16[32,4096]{1,0:T(8,128)(2,1)} %collective-permute-done.2.refs_0_), channel_id=1, source_target_pairs={{0,1},{8,9},{1,0},{9,8},{16,17},{24,25},{17,16},{25,24},{4,5},{12,... | collective-permute-start | bytes 786440 | tf_op jit(solution)/shard_map/ppermute | solution.py:207
  75.9 2.2 %collective-permute-start.4 = (bf16[32,4096]{1,0:T(8,128)(2,1)}, bf16[32,4096]{1,0:T(8,128)(2,1)}, u32[]{:S(2)}, u32[]{:S(2)}) collective-permute-start(bf16[32,4096]{1,0:T(8,128)(2,1)} %collective-permute-done.2.refs_0_), channel_id=1, source_target_pairs={{0,16},{8,24},{1,17},{9,25},{16,0},{24,8},{17,1},{25,9},{4,20},{12... | collective-permute-start | bytes 786440 | tf_op jit(solution)/shard_map/ppermute | solution.py:207
  78.8 2.4 %collective-permute-start.13 = (bf16[32,4096]{1,0:T(8,128)(2,1)S(1)}, bf16[32,4096]{1,0:T(8,128)(2,1)}, u32[]{:S(2)}, u32[]{:S(2)}) collective-permute-start(bf16[32,4096]{1,0:T(8,128)(2,1)S(1)} %collective-permute-done.10.refs_8_), channel_id=1, source_target_pairs={{0,17},{8,25},{1,16},{9,24},{16,1},{24,9},{17,0},{25,8},{4,21},{12... | collective-permute-start | bytes 786440 | tf_op jit(solution)/shard_map/ppermute | solution.py:207
  83.4 1.3 collective-permute-done.4.refs_2_
  84.7 1.5 collective-permute-start.8
  86.2 4.2 %collective-permute-done.5.refs_3_ = bf16[32,4096]{1,0:T(8,128)(2,1)} collective-permute-done((bf16[32,4096]{1,0:T(8,128)(2,1)}, bf16[32,4096]{1,0:T(8,128)(2,1)}, u32[]{:S(2)}, u32[]{:S(2)}) %collective-permute-start.5) | collective-permute-done | bytes 262176 | tf_op jit(solution)/shard_map/ppermute | solution.py:207
  91.8 3.5 %convert_element_type.50.refs_18_ = bf16[256,256]{1,0:T(8,128)(2,1)} reshape(bf16[32,8,32,8]{3,2,1,0:T(8,128)(2,1)S(1)} %multiply_convert_fusion) | data formatting | bytes 262144 | tf_op jit(solution)/shard_map/convert_element_type | solution.py:235
  95.4 4.4 %center_state.1.refs_19_ = bf16[256,4096]{1,0:T(8,128)(2,1)} custom-call(bf16[32,4096]{1,0:T(8,128)(2,1)} %copy-done, bf16[32,4096]{1,0:T(8,128)(2,1)} %copy-done.1, bf16[32,4096]{1,0:T(8,128)(2,1)} %copy-done.2, bf16[32,4096]{1,0:T(8,128)(2,1)} %copy-done.3, bf16[32,4096]{1,0:T(8,128)(2,1)} %copy-done.9, bf16[32,4096]{1,0:T(8,128)(2,1)} %copy-done.10, ...), custom_call_target="tpu_custom_call" | custom-call | flops 4194304 | bytes 4194304 | tf_op jit(solution)/shard_map/center_state/pallas_call | solution.py:86
  99.8 19.0 %update.1 = (bf16[32,4096]{1,0:T(8,128)(2,1)}, bf16[32,4096]{1,0:T(8,128)(2,1)}, bf16[32,4096]{1,0:T(8,128)(2,1)}, bf16[32,4096]{1,0:T(8,128)(2,1)}) custom-call(bf16[32,4096]{1,0:T(8,128)(2,1)} %collective-permute-done.2.refs_0_, bf16[32,4096]{1,0:T(8,128)(2,1)} %collective-permute-done.3.refs_1_, bf16[32,4096]{1,0:T(8,128)(2,1)} %collective-permute-done.4.refs_2_, ...), custom_call_target="tpu_custom_call" | custom-call | flops 1073741824 | bytes 9437184 | tf_op jit(solution)/shard_map/update/pallas_call | solution.py:154
  118.8 3.5 %collective-permute-start.24 = (bf16[32,4096]{1,0:T(8,128)(2,1)}, bf16[32,4096]{1,0:T(8,128)(2,1)S(1)}, u32[]{:S(2)}, u32[]{:S(2)}) collective-permute-start(bf16[32,4096]{1,0:T(8,128)(2,1)} %get-tuple-element.9), channel_id=1, source_target_pairs={{0,0},{8,1},{1,2},{9,3},{16,4},{24,5},{17,6},{25,7},{4,8},{12,9},{... | collective-permute-start | bytes 786440 | tf_op jit(solution)/shard_map/ppermute | solution.py:207
  122.3 3.7 %collective-permute-start.25 = (bf16[32,4096]{1,0:T(8,128)(2,1)}, bf16[32,4096]{1,0:T(8,128)(2,1)S(1)}, u32[]{:S(2)}, u32[]{:S(2)}) collective-permute-start(bf16[32,4096]{1,0:T(8,128)(2,1)} %get-tuple-element.10), channel_id=1, source_target_pairs={{1,0},{9,1},{0,2},{8,3},{17,4},{25,5},{16,6},{24,7},{5,8},{13,9},{... | collective-permute-start | bytes 786440 | tf_op jit(solution)/shard_map/ppermute | solution.py:207
  126.0 3.7 %collective-permute-start.26 = (bf16[32,4096]{1,0:T(8,128)(2,1)}, bf16[32,4096]{1,0:T(8,128)(2,1)S(1)}, u32[]{:S(2)}, u32[]{:S(2)}) collective-permute-start(bf16[32,4096]{1,0:T(8,128)(2,1)} %get-tuple-element.11), channel_id=1, source_target_pairs={{16,0},{24,1},{17,2},{25,3},{0,4},{8,5},{1,6},{9,7},{20,8},{28,9},... | collective-permute-start | bytes 786440 | tf_op jit(solution)/shard_map/ppermute | solution.py:207
  129.7 4.2 %collective-permute-start.27 = (bf16[32,4096]{1,0:T(8,128)(2,1)}, bf16[32,4096]{1,0:T(8,128)(2,1)S(1)}, u32[]{:S(2)}, u32[]{:S(2)}) collective-permute-start(bf16[32,4096]{1,0:T(8,128)(2,1)} %get-tuple-element.12), channel_id=1, source_target_pairs={{17,0},{25,1},{16,2},{24,3},{1,4},{9,5},{0,6},{8,7},{21,8},{29,9},... | collective-permute-start | bytes 786440 | tf_op jit(solution)/shard_map/ppermute | solution.py:207
  134.6 9.6 %collective-permute-done.26.refs_2_ = bf16[32,4096]{1,0:T(8,128)(2,1)S(1)} collective-permute-done((bf16[32,4096]{1,0:T(8,128)(2,1)}, bf16[32,4096]{1,0:T(8,128)(2,1)S(1)}, u32[]{:S(2)}, u32[]{:S(2)}) %collective-permute-start.26) | collective-permute-done | bytes 262176 | tf_op jit(solution)/shard_map/ppermute | solution.py:207
  144.2 5.5 %collective-permute-done.27.refs_3_ = bf16[32,4096]{1,0:T(8,128)(2,1)S(1)} collective-permute-done((bf16[32,4096]{1,0:T(8,128)(2,1)}, bf16[32,4096]{1,0:T(8,128)(2,1)S(1)}, u32[]{:S(2)}, u32[]{:S(2)}) %collective-permute-start.27) | collective-permute-done | bytes 262176 | tf_op jit(solution)/shard_map/ppermute | solution.py:207
  150.4 2.8 %place.1 = bf16[32,16384]{1,0:T(8,128)(2,1)} custom-call(s32[4]{0:T(128)} %pad_add_fusion.at, bf16[32,4096]{1,0:T(8,128)(2,1)} %copy-done.13, bf16[32,4096]{1,0:T(8,128)(2,1)} %copy-done.14, bf16[32,4096]{1,0:T(8,128)(2,1)} %copy-done.15, bf16[32,4096]{1,0:T(8,128)(2,1)} %copy-done.16), custom_call_target="tpu_custom_call" | custom-call | bytes 2097152 | tf_op jit(solution)/shard_map/place/pallas_call | solution.py:185
  (93 shorter events, 12.5 us)
Async XLA Ops:
  5.6 12.1 %collective-permute-start = (bf16[32,2,4096]{2,0,1:T(8,128)(2,1)}, bf16[32,2,4096]{2,0,1:T(8,128)(2,1)}, u32[]{:S(2)}, u32[]{:S(2)}) collective-permute-start(bf16[32,2,4096]{2,0,1:T(8,128)(2,1)} %bitcast.18), channel_id=1, source_target_pairs={{0,8},{1,9},{2,10},{3,11},{4,12},{5,13},{6,14},{7,15},{8,0},{9,1},... | collective-permute-start | bytes 1572872 | tf_op jit(solution)/shard_map/ppermute | solution.py:207
  6.4 37.3 %collective-permute-start.10 = (bf16[32,4096]{1,0:T(8,128)(2,1)}, bf16[32,4096]{1,0:T(8,128)(2,1)S(1)}, u32[]{:S(2)}, u32[]{:S(2)}) collective-permute-start(bf16[32,4096]{1,0:T(8,128)(2,1)} %convert_element_type.47), channel_id=1, source_target_pairs={{0,0},{1,8},{2,1},{3,9},{4,16},{5,24},{6,17},{7,25},{8,4},{9,12},{... | collective-permute-start | bytes 786440 | tf_op jit(solution)/shard_map/ppermute | solution.py:207
  12.4 5.3 %collective-permute-start.18 = (f32[8704]{0:T(1024)S(1)}, f32[8704]{0:T(1024)S(1)}, u32[]{:S(2)}, u32[]{:S(2)}) collective-permute-start(f32[8704]{0:T(1024)S(1)} %pad_maximum_fusion), channel_id=1, source_target_pairs={{0,0},{1,8},{2,1},{3,9},{4,16},{5,24},{6,17},{7,25},{8,4},{9,12},{... | collective-permute-start | bytes 104456 | tf_op jit(solution)/shard_map/ppermute | solution.py:207
  17.7 15.2 %collective-permute-start.19 = (f32[512]{0:T(512)S(1)}, f32[512]{0:T(512)S(1)}, u32[]{:S(2)}, u32[]{:S(2)}) collective-permute-start(f32[512]{0:T(512)S(1)} %slice.22), channel_id=1, source_target_pairs={{0,8},{1,9},{2,10},{3,11},{4,12},{5,13},{6,14},{7,15},{8,0},{9,1},... | collective-permute-start | bytes 6152 | tf_op jit(solution)/shard_map/ppermute | solution.py:207
  19.5 18.4 %collective-permute-start.1 = (bf16[32,4096]{1,0:T(8,128)(2,1)S(1)}, bf16[32,4096]{1,0:T(8,128)(2,1)}, u32[]{:S(2)}, u32[]{:S(2)}) collective-permute-start(bf16[32,4096]{1,0:T(8,128)(2,1)S(1)} %fusion.2), channel_id=1, source_target_pairs={{0,16},{1,17},{2,18},{3,19},{4,20},{5,21},{6,22},{7,23},{8,24},{9,... | collective-permute-start | bytes 786440 | tf_op jit(solution)/shard_map/ppermute | solution.py:207
  25.7 18.9 %collective-permute-start.14 = (bf16[32,4096]{1,0:T(8,128)(2,1)S(1)}, bf16[32,4096]{1,0:T(8,128)(2,1)S(1)}, u32[]{:S(2)}, u32[]{:S(2)}) collective-permute-start(bf16[32,4096]{1,0:T(8,128)(2,1)S(1)} %get-tuple-element.15), channel_id=1, source_target_pairs={{0,0},{1,8},{2,1},{3,9},{4,16},{5,24},{6,17},{7,25},{8,4},{9,12},{... | collective-permute-start | bytes 786440 | tf_op jit(solution)/shard_map/ppermute | solution.py:207
  30.0 33.1 %collective-permute-start.15 = (bf16[32,4096]{1,0:T(8,128)(2,1)}, bf16[32,4096]{1,0:T(8,128)(2,1)S(1)}, u32[]{:S(2)}, u32[]{:S(2)}) collective-permute-start(bf16[32,4096]{1,0:T(8,128)(2,1)} %get-tuple-element.14), channel_id=1, source_target_pairs={{0,1},{1,9},{2,0},{3,8},{4,17},{5,25},{6,16},{7,24},{8,5},{9,13},{... | collective-permute-start | bytes 786440 | tf_op jit(solution)/shard_map/ppermute | solution.py:207
  33.0 32.1 %collective-permute-start.16 = (bf16[32,4096]{1,0:T(8,128)(2,1)S(1)}, bf16[32,4096]{1,0:T(8,128)(2,1)S(1)}, u32[]{:S(2)}, u32[]{:S(2)}) collective-permute-start(bf16[32,4096]{1,0:T(8,128)(2,1)S(1)} %get-tuple-element.16), channel_id=1, source_target_pairs={{0,16},{1,24},{2,17},{3,25},{4,0},{5,8},{6,1},{7,9},{8,20},{9,28},... | collective-permute-start | bytes 786440 | tf_op jit(solution)/shard_map/ppermute | solution.py:207
  37.9 29.0 %collective-permute-start.17 = (bf16[32,4096]{1,0:T(8,128)(2,1)S(1)}, bf16[32,4096]{1,0:T(8,128)(2,1)S(1)}, u32[]{:S(2)}, u32[]{:S(2)}) collective-permute-start(bf16[32,4096]{1,0:T(8,128)(2,1)S(1)} %get-tuple-element.13), channel_id=1, source_target_pairs={{0,17},{1,25},{2,16},{3,24},{4,1},{5,9},{6,0},{7,8},{8,21},{9,29},... | collective-permute-start | bytes 786440 | tf_op jit(solution)/shard_map/ppermute | solution.py:207
  43.7 51.7 %copy-start.6 = (bf16[32,4096]{1,0:T(8,128)(2,1)}, bf16[32,4096]{1,0:T(8,128)(2,1)S(1)}, u32[]{:S(2)}) copy-start(bf16[32,4096]{1,0:T(8,128)(2,1)S(1)} %collective-permute-done.10.refs_8_) | copy-start | bytes 786436
  43.7 23.4 %collective-permute-start.11 = (bf16[32,4096]{1,0:T(8,128)(2,1)S(1)}, bf16[32,4096]{1,0:T(8,128)(2,1)S(1)}, u32[]{:S(2)}, u32[]{:S(2)}) collective-permute-start(bf16[32,4096]{1,0:T(8,128)(2,1)S(1)} %collective-permute-done.10.refs_8_), channel_id=1, source_target_pairs={{0,1},{8,9},{1,0},{9,8},{16,17},{24,25},{17,16},{25,24},{4,5},{12,... | collective-permute-start | bytes 786440 | tf_op jit(solution)/shard_map/ppermute | solution.py:207
  44.6 50.8 %copy-start = (bf16[32,4096]{1,0:T(8,128)(2,1)}, bf16[32,4096]{1,0:T(8,128)(2,1)S(1)}, u32[]{:S(2)}) copy-start(bf16[32,4096]{1,0:T(8,128)(2,1)S(1)} %collective-permute-done.14.refs_0_.refs_12_) | copy-start | bytes 786436
  44.6 22.9 %collective-permute-start.12 = (bf16[32,4096]{1,0:T(8,128)(2,1)S(1)}, bf16[32,4096]{1,0:T(8,128)(2,1)S(1)}, u32[]{:S(2)}, u32[]{:S(2)}) collective-permute-start(bf16[32,4096]{1,0:T(8,128)(2,1)S(1)} %collective-permute-done.10.refs_8_), channel_id=1, source_target_pairs={{0,16},{8,24},{1,17},{9,25},{16,0},{24,8},{17,1},{25,9},{4,20},{12... | collective-permute-start | bytes 786440 | tf_op jit(solution)/shard_map/ppermute | solution.py:207
  63.1 32.2 %copy-start.1 = (bf16[32,4096]{1,0:T(8,128)(2,1)}, bf16[32,4096]{1,0:T(8,128)(2,1)S(1)}, u32[]{:S(2)}) copy-start(bf16[32,4096]{1,0:T(8,128)(2,1)S(1)} %collective-permute-done.15.refs_1_.refs_13_) | copy-start | bytes 786436
  63.1 8.0 %collective-permute-start.2 = (bf16[32,4096]{1,0:T(8,128)(2,1)}, bf16[32,4096]{1,0:T(8,128)(2,1)}, u32[]{:S(2)}, u32[]{:S(2)}) collective-permute-start(bf16[32,4096]{1,0:T(8,128)(2,1)} %fusion.1), channel_id=1, source_target_pairs={{0,0},{1,8},{2,1},{3,9},{4,16},{5,24},{6,17},{7,25},{8,4},{9,12},{... | collective-permute-start | bytes 786440 | tf_op jit(solution)/shard_map/ppermute | solution.py:207
  65.1 30.3 %copy-start.2 = (bf16[32,4096]{1,0:T(8,128)(2,1)}, bf16[32,4096]{1,0:T(8,128)(2,1)S(1)}, u32[]{:S(2)}) copy-start(bf16[32,4096]{1,0:T(8,128)(2,1)S(1)} %collective-permute-done.16.refs_2_.refs_14_) | copy-start | bytes 786436
  65.1 10.8 %collective-permute-start.20 = (bf16[32,4096]{1,0:T(8,128)(2,1)S(1)}, bf16[32,4096]{1,0:T(8,128)(2,1)S(1)}, u32[]{:S(2)}, u32[]{:S(2)}) collective-permute-start(bf16[32,4096]{1,0:T(8,128)(2,1)S(1)} %collective-permute-done.14.refs_0_.refs_12_), channel_id=1, source_target_pairs={{0,8},{1,9},{2,10},{3,11},{4,12},{5,13},{6,14},{7,15},{8,0},{9,1},... | collective-permute-start | bytes 786440 | tf_op jit(solution)/shard_map/ppermute | solution.py:207
  66.9 11.2 %collective-permute-start.21 = (bf16[32,4096]{1,0:T(8,128)(2,1)S(1)}, bf16[32,4096]{1,0:T(8,128)(2,1)S(1)}, u32[]{:S(2)}, u32[]{:S(2)}) collective-permute-start(bf16[32,4096]{1,0:T(8,128)(2,1)S(1)} %collective-permute-done.15.refs_1_.refs_13_), channel_id=1, source_target_pairs={{0,8},{1,9},{2,10},{3,11},{4,12},{5,13},{6,14},{7,15},{8,0},{9,1},... | collective-permute-start | bytes 786440 | tf_op jit(solution)/shard_map/ppermute | solution.py:207
  67.1 11.7 %collective-permute-start.22 = (bf16[32,4096]{1,0:T(8,128)(2,1)S(1)}, bf16[32,4096]{1,0:T(8,128)(2,1)S(1)}, u32[]{:S(2)}, u32[]{:S(2)}) collective-permute-start(bf16[32,4096]{1,0:T(8,128)(2,1)S(1)} %collective-permute-done.16.refs_2_.refs_14_), channel_id=1, source_target_pairs={{0,8},{1,9},{2,10},{3,11},{4,12},{5,13},{6,14},{7,15},{8,0},{9,1},... | collective-permute-start | bytes 786440 | tf_op jit(solution)/shard_map/ppermute | solution.py:207
  67.5 13.7 %collective-permute-start.23 = (bf16[32,4096]{1,0:T(8,128)(2,1)S(1)}, bf16[32,4096]{1,0:T(8,128)(2,1)S(1)}, u32[]{:S(2)}, u32[]{:S(2)}) collective-permute-start(bf16[32,4096]{1,0:T(8,128)(2,1)S(1)} %collective-permute-done.17.refs_3_.refs_15_), channel_id=1, source_target_pairs={{0,8},{1,9},{2,10},{3,11},{4,12},{5,13},{6,14},{7,15},{8,0},{9,1},... | collective-permute-start | bytes 786440 | tf_op jit(solution)/shard_map/ppermute | solution.py:207
  71.1 11.7 %collective-permute-start.3 = (bf16[32,4096]{1,0:T(8,128)(2,1)}, bf16[32,4096]{1,0:T(8,128)(2,1)}, u32[]{:S(2)}, u32[]{:S(2)}) collective-permute-start(bf16[32,4096]{1,0:T(8,128)(2,1)} %collective-permute-done.2.refs_0_), channel_id=1, source_target_pairs={{0,1},{8,9},{1,0},{9,8},{16,17},{24,25},{17,16},{25,24},{4,5},{12,... | collective-permute-start | bytes 786440 | tf_op jit(solution)/shard_map/ppermute | solution.py:207
  75.9 8.9 %collective-permute-start.4 = (bf16[32,4096]{1,0:T(8,128)(2,1)}, bf16[32,4096]{1,0:T(8,128)(2,1)}, u32[]{:S(2)}, u32[]{:S(2)}) collective-permute-start(bf16[32,4096]{1,0:T(8,128)(2,1)} %collective-permute-done.2.refs_0_), channel_id=1, source_target_pairs={{0,16},{8,24},{1,17},{9,25},{16,0},{24,8},{17,1},{25,9},{4,20},{12... | collective-permute-start | bytes 786440 | tf_op jit(solution)/shard_map/ppermute | solution.py:207
  78.1 12.3 %collective-permute-start.5 = (bf16[32,4096]{1,0:T(8,128)(2,1)}, bf16[32,4096]{1,0:T(8,128)(2,1)}, u32[]{:S(2)}, u32[]{:S(2)}) collective-permute-start(bf16[32,4096]{1,0:T(8,128)(2,1)} %collective-permute-done.2.refs_0_), channel_id=1, source_target_pairs={{0,17},{8,25},{1,16},{9,24},{16,1},{24,9},{17,0},{25,8},{4,21},{12... | collective-permute-start | bytes 786440 | tf_op jit(solution)/shard_map/ppermute | solution.py:207
  78.8 21.0 %collective-permute-start.13 = (bf16[32,4096]{1,0:T(8,128)(2,1)S(1)}, bf16[32,4096]{1,0:T(8,128)(2,1)}, u32[]{:S(2)}, u32[]{:S(2)}) collective-permute-start(bf16[32,4096]{1,0:T(8,128)(2,1)S(1)} %collective-permute-done.10.refs_8_), channel_id=1, source_target_pairs={{0,17},{8,25},{1,16},{9,24},{16,1},{24,9},{17,0},{25,8},{4,21},{12... | collective-permute-start | bytes 786440 | tf_op jit(solution)/shard_map/ppermute | solution.py:207
  81.2 18.6 %collective-permute-start.6 = (bf16[32,4096]{1,0:T(8,128)(2,1)}, bf16[32,4096]{1,0:T(8,128)(2,1)}, u32[]{:S(2)}, u32[]{:S(2)}) collective-permute-start(bf16[32,4096]{1,0:T(8,128)(2,1)} %collective-permute-done.2.refs_0_), channel_id=1, source_target_pairs={{0,8},{1,9},{2,10},{3,11},{4,12},{5,13},{6,14},{7,15},{8,0},{9,1},... | collective-permute-start | bytes 786440 | tf_op jit(solution)/shard_map/ppermute | solution.py:207
  82.8 17.0 %collective-permute-start.7 = (bf16[32,4096]{1,0:T(8,128)(2,1)}, bf16[32,4096]{1,0:T(8,128)(2,1)}, u32[]{:S(2)}, u32[]{:S(2)}) collective-permute-start(bf16[32,4096]{1,0:T(8,128)(2,1)} %collective-permute-done.3.refs_1_), channel_id=1, source_target_pairs={{0,8},{1,9},{2,10},{3,11},{4,12},{5,13},{6,14},{7,15},{8,0},{9,1},... | collective-permute-start | bytes 786440 | tf_op jit(solution)/shard_map/ppermute | solution.py:207
  84.7 15.1 %collective-permute-start.8 = (bf16[32,4096]{1,0:T(8,128)(2,1)}, bf16[32,4096]{1,0:T(8,128)(2,1)}, u32[]{:S(2)}, u32[]{:S(2)}) collective-permute-start(bf16[32,4096]{1,0:T(8,128)(2,1)} %collective-permute-done.4.refs_2_), channel_id=1, source_target_pairs={{0,8},{1,9},{2,10},{3,11},{4,12},{5,13},{6,14},{7,15},{8,0},{9,1},... | collective-permute-start | bytes 786440 | tf_op jit(solution)/shard_map/ppermute | solution.py:207
  90.4 9.4 %collective-permute-start.9 = (bf16[32,4096]{1,0:T(8,128)(2,1)}, bf16[32,4096]{1,0:T(8,128)(2,1)}, u32[]{:S(2)}, u32[]{:S(2)}) collective-permute-start(bf16[32,4096]{1,0:T(8,128)(2,1)} %collective-permute-done.5.refs_3_), channel_id=1, source_target_pairs={{0,8},{1,9},{2,10},{3,11},{4,12},{5,13},{6,14},{7,15},{8,0},{9,1},... | collective-permute-start | bytes 786440 | tf_op jit(solution)/shard_map/ppermute | solution.py:207
  118.8 15.7 %collective-permute-start.24 = (bf16[32,4096]{1,0:T(8,128)(2,1)}, bf16[32,4096]{1,0:T(8,128)(2,1)S(1)}, u32[]{:S(2)}, u32[]{:S(2)}) collective-permute-start(bf16[32,4096]{1,0:T(8,128)(2,1)} %get-tuple-element.9), channel_id=1, source_target_pairs={{0,0},{8,1},{1,2},{9,3},{16,4},{24,5},{17,6},{25,7},{4,8},{12,9},{... | collective-permute-start | bytes 786440 | tf_op jit(solution)/shard_map/ppermute | solution.py:207
  122.3 12.3 %collective-permute-start.25 = (bf16[32,4096]{1,0:T(8,128)(2,1)}, bf16[32,4096]{1,0:T(8,128)(2,1)S(1)}, u32[]{:S(2)}, u32[]{:S(2)}) collective-permute-start(bf16[32,4096]{1,0:T(8,128)(2,1)} %get-tuple-element.10), channel_id=1, source_target_pairs={{1,0},{9,1},{0,2},{8,3},{17,4},{25,5},{16,6},{24,7},{5,8},{13,9},{... | collective-permute-start | bytes 786440 | tf_op jit(solution)/shard_map/ppermute | solution.py:207
  126.0 18.2 %collective-permute-start.26 = (bf16[32,4096]{1,0:T(8,128)(2,1)}, bf16[32,4096]{1,0:T(8,128)(2,1)S(1)}, u32[]{:S(2)}, u32[]{:S(2)}) collective-permute-start(bf16[32,4096]{1,0:T(8,128)(2,1)} %get-tuple-element.11), channel_id=1, source_target_pairs={{16,0},{24,1},{17,2},{25,3},{0,4},{8,5},{1,6},{9,7},{20,8},{28,9},... | collective-permute-start | bytes 786440 | tf_op jit(solution)/shard_map/ppermute | solution.py:207
  129.7 20.0 %collective-permute-start.27 = (bf16[32,4096]{1,0:T(8,128)(2,1)}, bf16[32,4096]{1,0:T(8,128)(2,1)S(1)}, u32[]{:S(2)}, u32[]{:S(2)}) collective-permute-start(bf16[32,4096]{1,0:T(8,128)(2,1)} %get-tuple-element.12), channel_id=1, source_target_pairs={{17,0},{25,1},{16,2},{24,3},{1,4},{9,5},{0,6},{8,7},{21,8},{29,9},... | collective-permute-start | bytes 786440 | tf_op jit(solution)/shard_map/ppermute | solution.py:207
  (18 other events, 215.1 us)

commit v2 on v1

--- a/solution.py
+++ b/solution.py
@@ -9,6 +9,7 @@
 
 OB = 128
 SUB = 8
+UNROLL = 8
 AXES = ("vox", "mem")
 BF = jnp.bfloat16
 F32 = jnp.float32
@@ -61,6 +62,10 @@
     return pl.CostEstimate(flops=flops, bytes_accessed=moved, transcendentals=0)
 
 
+def grant(needed):
+    return needed + needed // 8 + (2 << 20)
+
+
 def vmem(count):
     return [pl.BlockSpec(memory_space=pltpu.VMEM)] * count
 
@@ -77,7 +82,7 @@
         out[:, cols] = jnp.concatenate([x - mean for x in values], axis=0).astype(BF)
         return carry
 
-    lax.fori_loop(0, width // OB, step, 0)
+    lax.fori_loop(0, width // OB, step, 0, unroll=4)
 
 
 def center_state(pieces):
@@ -89,6 +94,7 @@
         in_specs=vmem(len(pieces)),
         out_specs=vmem(1)[0],
         cost_estimate=cost(4 * total * width, 4 * total * width),
+        compiler_params=pltpu.CompilerParams(vmem_limit_bytes=grant(4 * total * width)),
         name="center_state",
     )(*pieces)
 
@@ -112,13 +118,13 @@
         theirs = jnp.concatenate([r[:, cols].astype(F32) for r in other], axis=0)
         noise = jnp.concatenate([r[:, cols].astype(F32) for r in pert], axis=0)
         mean = (jnp.sum(mine, axis=0, keepdims=True) + jnp.sum(theirs, axis=0, keepdims=True)) * (1.0 / count)
-        weights = ((obs[:, cols] + noise - mine) / var[:, cols]).astype(BF)
+        weights = ((obs[:, cols] + noise - mine) * (1.0 / var[:, cols])).astype(BF)
         anomaly = jnp.concatenate([mine - mean, theirs - mean], axis=0).astype(BF)
         m = lax.dot_general(weights, anomaly, (((1,), (1,)), ((), ())), preferred_element_type=F32)
         stacked[:, pl.ds(pl.multiple_of(o * SUB, SUB), SUB), :] = m.reshape(tiles, SUB, count)
         return carry
 
-    lax.fori_loop(0, groups, moment, 0)
+    lax.fori_loop(0, groups, moment, 0, unroll=UNROLL)
 
     def combine(g, carry):
         c = lax.dot_general(
@@ -127,7 +133,7 @@
         combined[:, pl.ds(pl.multiple_of(g * SUB, SUB), SUB), :] = c.reshape(blocks, SUB, count)
         return carry
 
-    lax.fori_loop(0, tiles, combine, 0)
+    lax.fori_loop(0, tiles, combine, 0, unroll=UNROLL)
 
     cells = anom.shape[1] // blocks
 
@@ -141,7 +147,7 @@
             outs[i][:, cols] = new.astype(BF)
         return carry
 
-    lax.fori_loop(0, blocks, increment, 0)
+    lax.fori_loop(0, blocks, increment, 0, unroll=UNROLL)
 
 
 def update(own, other, pert, state, obs, var, kron, anom, blocks):
@@ -151,6 +157,8 @@
     count, lanes = 2 * n * rows, n * rows
     groups = data // OB
     flops = 2 * lanes * count * (data + kron.shape[0] * groups * SUB // SUB + cells)
+    held = 2 * (3 * lanes * data + 2 * lanes * cells + count * cells + kron.size) + 64 * data
+    held += 4 * lanes * count * (groups + blocks)
     return pl.pallas_call(
         functools.partial(update_kernel, n),
         out_shape=[jax.ShapeDtypeStruct((rows, cells), BF)] * n,
@@ -161,7 +169,7 @@
             pltpu.VMEM((blocks, lanes, count), F32),
         ],
         cost_estimate=cost(flops, 2 * (3 * lanes * data + 3 * count * cells)),
-        compiler_params=pltpu.CompilerParams(vmem_limit_bytes=60 << 20),
+        compiler_params=pltpu.CompilerParams(vmem_limit_bytes=grant(held)),
         name="update",
     )(*own, *other, *pert, *state, obs, var, kron, anom)
 
@@ -186,12 +194,13 @@
         functools.partial(place_kernel, n),
         grid_spec=pltpu.PrefetchScalarGridSpec(
             num_scalar_prefetch=1,
-            in_specs=vmem(n),
+            in_specs=[pl.BlockSpec(memory_space=pl.ANY)] * n,
             out_specs=pl.BlockSpec(memory_space=pl.ANY),
             scratch_shapes=[pltpu.SemaphoreType.DMA((n,))],
         ),
         out_shape=jax.ShapeDtypeStruct((rows, n * width), BF),
         cost_estimate=cost(0, 4 * n * rows * width),
+        compiler_params=pltpu.CompilerParams(vmem_limit_bytes=2 << 20),
         name="place",
     )(at, *pieces)
 
@@ -206,14 +215,21 @@
     def send(value, pairs):
         return lax.ppermute(value, AXES, pairs)
 
-    parts = partials[0].reshape(rows, half, 2, data)
-    away = lax.dynamic_slice_in_dim(parts, 1 - core, 1, 2)[:, :, 0].astype(BF)
+    def chip(i):
+        return plan.moved(m // 2, i)
+
+    def part(group_x, group_core):
+        return lax.dynamic_slice_in_dim(partials[0], (group_x * 2 + group_core) * data, data, 1)
+
+    away = jnp.concatenate([part(k, 1 - core).astype(BF) for k in range(half)], axis=0)
     got = send(away, plan.core())
-    pair = lax.dynamic_slice_in_dim(parts, core, 1, 2)[:, :, 0] + got.astype(F32)
-    total = lax.dynamic_slice_in_dim(pair, x, 1, 1)[:, 0]
+
+    def pair(group_x):
+        return part(group_x, core) + lax.dynamic_slice_in_dim(got, group_x * rows, rows, 0).astype(F32)
+
+    total = pair(x)
     for s in range(1, half):
-        piece = lax.dynamic_slice_in_dim(pair, (x + s) % half, 1, 1)[:, 0].astype(BF)
-        total = total + send(piece, plan.x_shift(s)).astype(F32)
+        total = total + send(pair((x + s) % half).astype(BF), plan.x_shift(s)).astype(F32)
     predicted = total.astype(BF)
 
     groups = data // OB
@@ -223,33 +239,29 @@
     tapers = jnp.sum(table_hits * taper_table[None, None, :], axis=2)
     picks = (obs_lists[:, :, None] == jnp.arange(groups, dtype=jnp.int32)[None, None, :]).astype(F32)
     coeff = jnp.sum(tapers[:, :, None] * picks, axis=1)
-    own_blocks = coeff.shape[0]
     first = plan.out_to_plane(0)
     small = send(jnp.concatenate([observed, variance, coeff.reshape(-1)]), first)
     obs, var = small[:data].reshape(1, data), small[data : 2 * data].reshape(1, data)
     mine = small[2 * data :]
     theirs = send(mine, plan.core())
+    blocks = 2 * coeff.shape[0]
     coeff = jnp.where(core == 0, jnp.concatenate([mine, theirs]), jnp.concatenate([theirs, mine]))
-    blocks = 2 * own_blocks
     coeff = coeff.reshape(blocks, groups)
     kron = (coeff[:, None, :, None] * jnp.eye(SUB, dtype=F32)[None, :, None, :]).astype(BF)
     kron = kron.reshape(blocks * SUB, groups * SUB)
 
-    def chip(i):
-        return plan.moved(m // 2, i)
-
-    own_state = [
-        send(lax.dynamic_slice_in_dim(ensemble, chip(i) * per_chip, per_chip, 1), plan.out_to_plane(i))
-        for i in range(n)
-    ]
-    other_state = [send(s, plan.core()) for s in own_state]
+    def cells_of(q):
+        return lax.dynamic_slice_in_dim(ensemble, q * per_chip, per_chip, 1)
+
+    own_state = [send(cells_of(chip(i)), plan.out_to_plane(i)) for i in range(n)]
+    other_state = [send(own_state[i], plan.core()) for i in range(n)]
     anom = center_state(own_state + other_state)
 
-    noise = send(perturb.astype(BF), first)
-    pert = [noise] + [send(noise, plan.in_plane(i)) for i in range(1, n)]
-    arrived = send(predicted, first)
-    own = [arrived] + [send(arrived, plan.in_plane(i)) for i in range(1, n)]
-    other = [send(p, plan.core()) for p in own]
+    pert = [send(perturb.astype(BF), first)]
+    pert += [send(pert[0], plan.in_plane(i)) for i in range(1, n)]
+    own = [send(predicted, first)]
+    own += [send(own[0], plan.in_plane(i)) for i in range(1, n)]
+    other = [send(own[i], plan.core()) for i in range(n)]
 
     new = update(own, other, pert, own_state, obs, var, kron, anom, blocks)
     back = [send(new[i], plan.back(i)) for i in range(n)]
@@ -257,10 +269,14 @@
     return place(back, at)
 
 
+def whole(plan, *args):
+    return local(plan, *args)
+
+
 def solution(mesh):
     plan = Plan(mesh.shape["vox"], mesh.shape["mem"])
     return jax.shard_map(
-        functools.partial(local, plan),
+        functools.partial(whole, plan),
         mesh=mesh,
         in_specs=(
             P("mem", "vox"),

time: 154 us -> 131 us (0.85)
  Pallas kernels: 26.3 us -> 9.66 us
  starting transfers between devices: 66.4 us -> 58.7 us
  local copies, waits for them, and re-layouts: 12.6 us -> 7.36 us
  waiting for transfers between devices: 41.7 us -> 45.5 us
  other arithmetic: 5.54 us -> 8.31 us
    pallas_call x1, Pallas kernels: 19 us -> 5.72 us  [update(): pl.pallas_call(functools.partial(update_kernel, n), out_shape=[jax.ShapeD...]
    ppermute x28, starting transfers between devices: 66.4 us -> 58.7 us  [send(): return lax.ppermute(value, AXES, pairs)]
    ppermute x28, waiting for transfers between devices: 41.7 us -> 45.5 us  [send(): return lax.ppermute(value, AXES, pairs)]
    another operation x1 -> x0, local copies, waits for them, and re-layouts: 3.03 us -> none  [local(): parts = partials[0].reshape(rows, half, 2, data)]
    convert_element_type x1 -> x2, other arithmetic: 0.74 us -> 3.48 us  [the longest x1 1.77 us: local(): pert = [send(perturb.astype(BF), first)]]
    unnamed x45 -> x16, local copies, waits for them, and re-layouts: 2.18 us -> 0.03 us
    pallas_call x1, Pallas kernels: 4.42 us -> 2.4 us  [center_state(): pl.pallas_call(functools.partial(center_kernel, len(pieces)), out_shape=j...]
    dynamic_slice x3 -> x1, local copies, waits for them, and re-layouts: 3.03 us -> 1.02 us  [cells_of(): return lax.dynamic_slice_in_dim(ensemble, q * per_chip, per_chip, 1)]
  transfers between devices with their start and end apart: 28 -> 28, of which waited for: 8 -> 8; matrix products, arithmetic and copies ran while one was open for 8% -> 10% of each run, Pallas kernels for 3% -> 2%
where the time goes in v2:
time: 131 us; the launch traced here: 130 us
  starting transfers between devices  58.7 us (45%)
  waiting for transfers between devices  45.5 us (35%)
  Pallas kernels  9.66 us (7%)
  other arithmetic  8.31 us (6%)
  local copies, waits for them, and re-layouts  7.36 us (6%)
    ppermute x28, starting transfers between devices, send(): return lax.ppermute(value, AXES, pairs)  58.7 us
    ppermute x28, waiting for transfers between devices, send(): return lax.ppermute(value, AXES, pairs)  45.5 us
    pallas_call x1, Pallas kernels, update(): pl.pallas_call(functools.partial(update_kernel, n), out_shape=[jax.ShapeD...  5.72 us
    convert_element_type x1, local copies, waits for them, and re-layouts, local(): (coeff[:, None, :, None] * jnp.eye(SUB, dtype=F32)[None, :, None, :]).ast...  4.05 us
  transfers between devices with their start and end apart: 28, of which 8 were waited for; matrix products, arithmetic and copies ran while one was open for 10% of the time, Pallas kernels for 2%

profile of v2, /device:TPU:1, one launch (start us, length us, event | category | flops | bytes accessed | tf_op | source)
XLA Modules:
  0.0 130.0 jit_solution(12683293016435029157)
XLA Ops:
  2.8 5.6 %collective-permute-start.18 = (f32[8704]{0:T(1024)S(1)}, f32[8704]{0:T(1024)S(1)}, u32[]{:S(2)}, u32[]{:S(2)}) collective-permute-start(f32[8704]{0:T(1024)S(1)} %pad_maximum_fusion.1), channel_id=1, source_target_pairs={{0,0},{1,8},{2,1},{3,9},{4,16},{5,24},{6,17},{7,25},{8,4},{9,12},{... | collective-permute-start | bytes 104456 | tf_op jit(solution)/shard_map/ppermute | solution.py:216
  8.4 1.8 %convert_element_type.55 = bf16[32,4096]{1,0:T(8,128)(2,1)} convert(f32[32,4096]{1,0:T(8,128)} %param.10) | non-fusion elementwise | flops 131072 | bytes 786432 | tf_op jit(solution)/shard_map/convert_element_type | solution.py:260
  10.2 3.2 %collective-permute-start.10 = (bf16[32,4096]{1,0:T(8,128)(2,1)}, bf16[32,4096]{1,0:T(8,128)(2,1)S(1)}, u32[]{:S(2)}, u32[]{:S(2)}) collective-permute-start(bf16[32,4096]{1,0:T(8,128)(2,1)} %convert_element_type.55), channel_id=1, source_target_pairs={{0,0},{1,8},{2,1},{3,9},{4,16},{5,24},{6,17},{7,25},{8,4},{9,12},{... | collective-permute-start | bytes 786440 | tf_op jit(solution)/shard_map/ppermute | solution.py:216
  13.6 1.7 %fusion = bf16[32,4096]{1,0:T(8,128)(2,1)} fusion(f32[1,32,16384]{2,1,0:T(8,128)S(1)} %copy-done.1, s32[]{:T(128)S(6)} %select_n.149, bf16[64,4096]{1,0:T(8,128)(2,1)} %collective-permute-done, s32[]{:T(128)S(6)} %select_n.150), kind=kLoop, calls=%fused_computation.3 | loop fusion | flops 393216 | bytes 1048584 | tf_op jit(solution)/shard_map/convert_element_type | solution.py:232
  15.3 2.2 %collective-permute-start.1 = (bf16[32,4096]{1,0:T(8,128)(2,1)}, bf16[32,4096]{1,0:T(8,128)(2,1)}, u32[]{:S(2)}, u32[]{:S(2)}) collective-permute-start(bf16[32,4096]{1,0:T(8,128)(2,1)} %fusion), channel_id=1, source_target_pairs={{0,16},{1,17},{2,18},{3,19},{4,20},{5,21},{6,22},{7,23},{8,24},{9,... | collective-permute-start | bytes 786440 | tf_op jit(solution)/shard_map/ppermute | solution.py:216
  18.6 3.6 %collective-permute-start.14 = (bf16[32,4096]{1,0:T(8,128)(2,1)}, bf16[32,4096]{1,0:T(8,128)(2,1)S(1)}, u32[]{:S(2)}, u32[]{:S(2)}) collective-permute-start(bf16[32,4096]{1,0:T(8,128)(2,1)} %get-tuple-element.17), channel_id=1, source_target_pairs={{0,0},{1,8},{2,1},{3,9},{4,16},{5,24},{6,17},{7,25},{8,4},{9,12},{... | collective-permute-start | bytes 786440 | tf_op jit(solution)/shard_map/ppermute | solution.py:216
  22.2 3.4 %collective-permute-start.15 = (bf16[32,4096]{1,0:T(8,128)(2,1)}, bf16[32,4096]{1,0:T(8,128)(2,1)S(1)}, u32[]{:S(2)}, u32[]{:S(2)}) collective-permute-start(bf16[32,4096]{1,0:T(8,128)(2,1)} %get-tuple-element.16), channel_id=1, source_target_pairs={{0,1},{1,9},{2,0},{3,8},{4,17},{5,25},{6,16},{7,24},{8,5},{9,13},{... | collective-permute-start | bytes 786440 | tf_op jit(solution)/shard_map/ppermute | solution.py:216
  25.7 4.0 %collective-permute-start.16 = (bf16[32,4096]{1,0:T(8,128)(2,1)}, bf16[32,4096]{1,0:T(8,128)(2,1)S(1)}, u32[]{:S(2)}, u32[]{:S(2)}) collective-permute-start(bf16[32,4096]{1,0:T(8,128)(2,1)} %get-tuple-element.18), channel_id=1, source_target_pairs={{0,16},{1,24},{2,17},{3,25},{4,0},{5,8},{6,1},{7,9},{8,20},{9,28},... | collective-permute-start | bytes 786440 | tf_op jit(solution)/shard_map/ppermute | solution.py:216
  29.7 8.5 %collective-permute-done.1 = bf16[32,4096]{1,0:T(8,128)(2,1)} collective-permute-done((bf16[32,4096]{1,0:T(8,128)(2,1)}, bf16[32,4096]{1,0:T(8,128)(2,1)}, u32[]{:S(2)}, u32[]{:S(2)}) %collective-permute-start.1) | collective-permute-done | bytes 262176 | tf_op jit(solution)/shard_map/ppermute | solution.py:216
  38.2 1.9 %collective-permute-start.17 = (bf16[32,4096]{1,0:T(8,128)(2,1)}, bf16[32,4096]{1,0:T(8,128)(2,1)S(1)}, u32[]{:S(2)}, u32[]{:S(2)}) collective-permute-start(bf16[32,4096]{1,0:T(8,128)(2,1)} %get-tuple-element.15), channel_id=1, source_target_pairs={{0,17},{1,25},{2,16},{3,24},{4,1},{5,9},{6,0},{7,8},{8,21},{9,29},... | collective-permute-start | bytes 786440 | tf_op jit(solution)/shard_map/ppermute | solution.py:216
  40.1 1.8 %fusion.2 = bf16[32,4096]{1,0:T(8,128)(2,1)} fusion(bf16[32,4096]{1,0:T(8,128)(2,1)} %collective-permute-done.1, f32[1,32,16384]{2,1,0:T(8,128)S(1)} %copy-done.1, s32[]{:T(128)S(6)} %select_n.144, bf16[64,4096]{1,0:T(8,128)(2,1)} %collective-permute-done, s32[]{:T(128)S(6)} %select_n.147), kind=kLoop, calls=%fused_computation.6 | loop fusion | flops 655360 | bytes 1310728 | tf_op jit(solution)/shard_map/convert_element_type | solution.py:233
  41.9 2.9 %collective-permute-start.11 = (bf16[32,4096]{1,0:T(8,128)(2,1)S(1)}, bf16[32,4096]{1,0:T(8,128)(2,1)S(1)}, u32[]{:S(2)}, u32[]{:S(2)}) collective-permute-start(bf16[32,4096]{1,0:T(8,128)(2,1)S(1)} %collective-permute-done.10.refs_8_), channel_id=1, source_target_pairs={{0,1},{8,9},{1,0},{9,8},{16,17},{24,25},{17,16},{25,24},{4,5},{12,... | collective-permute-start | bytes 786440 | tf_op jit(solution)/shard_map/ppermute | solution.py:216
  44.9 2.2 %collective-permute-start.12 = (bf16[32,4096]{1,0:T(8,128)(2,1)S(1)}, bf16[32,4096]{1,0:T(8,128)(2,1)S(1)}, u32[]{:S(2)}, u32[]{:S(2)}) collective-permute-start(bf16[32,4096]{1,0:T(8,128)(2,1)S(1)} %collective-permute-done.10.refs_8_), channel_id=1, source_target_pairs={{0,16},{8,24},{1,17},{9,25},{16,0},{24,8},{17,1},{25,9},{4,20},{12... | collective-permute-start | bytes 786440 | tf_op jit(solution)/shard_map/ppermute | solution.py:216
  47.1 6.0 %collective-permute-done.15.refs_1_.refs_13_ = bf16[32,4096]{1,0:T(8,128)(2,1)S(1)} collective-permute-done((bf16[32,4096]{1,0:T(8,128)(2,1)}, bf16[32,4096]{1,0:T(8,128)(2,1)S(1)}, u32[]{:S(2)}, u32[]{:S(2)}) %collective-permute-start.15) | collective-permute-done | bytes 262176 | tf_op jit(solution)/shard_map/ppermute | solution.py:216
  53.1 1.9 %collective-permute-start.2 = (bf16[32,4096]{1,0:T(8,128)(2,1)}, bf16[32,4096]{1,0:T(8,128)(2,1)S(1)}, u32[]{:S(2)}, u32[]{:S(2)}) collective-permute-start(bf16[32,4096]{1,0:T(8,128)(2,1)} %fusion.2), channel_id=1, source_target_pairs={{0,0},{1,8},{2,1},{3,9},{4,16},{5,24},{6,17},{7,25},{8,4},{9,12},{... | collective-permute-start | bytes 786440 | tf_op jit(solution)/shard_map/ppermute | solution.py:216
  56.5 8.0 %collective-permute-done.12.refs_10_ = bf16[32,4096]{1,0:T(8,128)(2,1)S(1)} collective-permute-done((bf16[32,4096]{1,0:T(8,128)(2,1)S(1)}, bf16[32,4096]{1,0:T(8,128)(2,1)S(1)}, u32[]{:S(2)}, u32[]{:S(2)}) %collective-permute-start.12) | collective-permute-done | bytes 262176 | tf_op jit(solution)/shard_map/ppermute | solution.py:216
  64.4 2.2 %collective-permute-start.23 = (bf16[32,4096]{1,0:T(8,128)(2,1)S(1)}, bf16[32,4096]{1,0:T(8,128)(2,1)}, u32[]{:S(2)}, u32[]{:S(2)}) collective-permute-start(bf16[32,4096]{1,0:T(8,128)(2,1)S(1)} %collective-permute-done.17.refs_3_.refs_15_), channel_id=1, source_target_pairs={{0,8},{1,9},{2,10},{3,11},{4,12},{5,13},{6,14},{7,15},{8,0},{9,1},... | collective-permute-start | bytes 786440 | tf_op jit(solution)/shard_map/ppermute | solution.py:216
  67.3 1.8 %collective-permute-start.4 = (bf16[32,4096]{1,0:T(8,128)(2,1)S(1)}, bf16[32,4096]{1,0:T(8,128)(2,1)S(1)}, u32[]{:S(2)}, u32[]{:S(2)}) collective-permute-start(bf16[32,4096]{1,0:T(8,128)(2,1)S(1)} %collective-permute-done.2.refs_0_), channel_id=1, source_target_pairs={{0,16},{8,24},{1,17},{9,25},{16,0},{24,8},{17,1},{25,9},{4,20},{12... | collective-permute-start | bytes 786440 | tf_op jit(solution)/shard_map/ppermute | solution.py:216
  75.4 2.8 %collective-permute-start.8 = (bf16[32,4096]{1,0:T(8,128)(2,1)S(1)}, bf16[32,4096]{1,0:T(8,128)(2,1)}, u32[]{:S(2)}, u32[]{:S(2)}) collective-permute-start(bf16[32,4096]{1,0:T(8,128)(2,1)S(1)} %collective-permute-done.4.refs_2_), channel_id=1, source_target_pairs={{0,8},{1,9},{2,10},{3,11},{4,12},{5,13},{6,14},{7,15},{8,0},{9,1},... | collective-permute-start | bytes 786440 | tf_op jit(solution)/shard_map/ppermute | solution.py:216
  78.1 3.9 %collective-permute-done.5.refs_3_ = bf16[32,4096]{1,0:T(8,128)(2,1)S(1)} collective-permute-done((bf16[32,4096]{1,0:T(8,128)(2,1)S(1)}, bf16[32,4096]{1,0:T(8,128)(2,1)S(1)}, u32[]{:S(2)}, u32[]{:S(2)}) %collective-permute-start.5) | collective-permute-done | bytes 262176 | tf_op jit(solution)/shard_map/ppermute | solution.py:216
  83.4 1.8 %multiply_convert_fusion = bf16[32,8,32,8]{3,2,1,0:T(8,128)(2,1)} fusion(f32[8,8]{1,0:T(8,128)S(1)} %fusion.5, f32[32,32]{1,0:T(8,128)S(1)} %maximum_select_fusion), kind=kLoop, calls=%fused_computation | loop fusion | flops 131072 | bytes 135424 | tf_op jit(solution)/shard_map/convert_element_type | solution.py:250
  85.1 4.1 %convert_element_type.58.refs_18_ = bf16[256,256]{1,0:T(8,128)(2,1)S(1)} reshape(bf16[32,8,32,8]{3,2,1,0:T(8,128)(2,1)} %multiply_convert_fusion) | data formatting | bytes 262144 | tf_op jit(solution)/shard_map/convert_element_type | solution.py:250
  89.2 2.4 %center_state.1.refs_19_ = bf16[256,4096]{1,0:T(8,128)(2,1)S(1)} custom-call(bf16[32,4096]{1,0:T(8,128)(2,1)S(1)} %collective-permute-done.14.refs_0_.refs_12_, bf16[32,4096]{1,0:T(8,128)(2,1)S(1)} %collective-permute-done.15.refs_1_.refs_13_, bf16[32,4096]{1,0:T(8,128)(2,1)S(1)} %collective-permute-done.16.refs_2_.refs_14_, ...), custom_call_target="tpu_custom_call" | custom-call | flops 4194304 | bytes 4194304 | tf_op jit(solution)/shard_map/center_state/pallas_call | solution.py:91
  91.7 5.7 %update.1 = (bf16[32,4096]{1,0:T(8,128)(2,1)S(1)}, bf16[32,4096]{1,0:T(8,128)(2,1)S(1)}, bf16[32,4096]{1,0:T(8,128)(2,1)S(1)}, bf16[32,4096]{1,0:T(8,128)(2,1)S(1)}) custom-call(bf16[32,4096]{1,0:T(8,128)(2,1)S(1)} %collective-permute-done.2.refs_0_, bf16[32,4096]{1,0:T(8,128)(2,1)S(1)} %collective-permute-done.3.refs_1_, ...), custom_call_target="tpu_custom_call" | custom-call | flops 1073741824 | bytes 9437184 | tf_op jit(solution)/shard_map/update/pallas_call | solution.py:162
  97.4 3.4 %collective-permute-start.24 = (bf16[32,4096]{1,0:T(8,128)(2,1)S(1)}, bf16[32,4096]{1,0:T(8,128)(2,1)S(1)}, u32[]{:S(2)}, u32[]{:S(2)}) collective-permute-start(bf16[32,4096]{1,0:T(8,128)(2,1)S(1)} %get-tuple-element.9), channel_id=1, source_target_pairs={{0,0},{8,1},{1,2},{9,3},{16,4},{24,5},{17,6},{25,7},{4,8},{12,9},{... | collective-permute-start | bytes 786440 | tf_op jit(solution)/shard_map/ppermute | solution.py:216
  100.8 4.2 %collective-permute-start.25 = (bf16[32,4096]{1,0:T(8,128)(2,1)S(1)}, bf16[32,4096]{1,0:T(8,128)(2,1)S(1)}, u32[]{:S(2)}, u32[]{:S(2)}) collective-permute-start(bf16[32,4096]{1,0:T(8,128)(2,1)S(1)} %get-tuple-element.10), channel_id=1, source_target_pairs={{1,0},{9,1},{0,2},{8,3},{17,4},{25,5},{16,6},{24,7},{5,8},{13,9},{... | collective-permute-start | bytes 786440 | tf_op jit(solution)/shard_map/ppermute | solution.py:216
  105.0 3.1 %collective-permute-start.26 = (bf16[32,4096]{1,0:T(8,128)(2,1)S(1)}, bf16[32,4096]{1,0:T(8,128)(2,1)S(1)}, u32[]{:S(2)}, u32[]{:S(2)}) collective-permute-start(bf16[32,4096]{1,0:T(8,128)(2,1)S(1)} %get-tuple-element.11), channel_id=1, source_target_pairs={{16,0},{24,1},{17,2},{25,3},{0,4},{8,5},{1,6},{9,7},{20,8},{28,9},... | collective-permute-start | bytes 786440 | tf_op jit(solution)/shard_map/ppermute | solution.py:216
  108.2 2.5 %collective-permute-start.27 = (bf16[32,4096]{1,0:T(8,128)(2,1)S(1)}, bf16[32,4096]{1,0:T(8,128)(2,1)S(1)}, u32[]{:S(2)}, u32[]{:S(2)}) collective-permute-start(bf16[32,4096]{1,0:T(8,128)(2,1)S(1)} %get-tuple-element.12), channel_id=1, source_target_pairs={{17,0},{25,1},{16,2},{24,3},{1,4},{9,5},{0,6},{8,7},{21,8},{29,9},... | collective-permute-start | bytes 786440 | tf_op jit(solution)/shard_map/ppermute | solution.py:216
  110.8 3.4 %collective-permute-done.25.refs_1_ = bf16[32,4096]{1,0:T(8,128)(2,1)S(1)} collective-permute-done((bf16[32,4096]{1,0:T(8,128)(2,1)S(1)}, bf16[32,4096]{1,0:T(8,128)(2,1)S(1)}, u32[]{:S(2)}, u32[]{:S(2)}) %collective-permute-start.25) | collective-permute-done | bytes 262176 | tf_op jit(solution)/shard_map/ppermute | solution.py:216
  114.2 7.3 %collective-permute-done.26.refs_2_ = bf16[32,4096]{1,0:T(8,128)(2,1)S(1)} collective-permute-done((bf16[32,4096]{1,0:T(8,128)(2,1)S(1)}, bf16[32,4096]{1,0:T(8,128)(2,1)S(1)}, u32[]{:S(2)}, u32[]{:S(2)}) %collective-permute-start.26) | collective-permute-done | bytes 262176 | tf_op jit(solution)/shard_map/ppermute | solution.py:216
  121.5 7.0 %collective-permute-done.27.refs_3_ = bf16[32,4096]{1,0:T(8,128)(2,1)S(1)} collective-permute-done((bf16[32,4096]{1,0:T(8,128)(2,1)S(1)}, bf16[32,4096]{1,0:T(8,128)(2,1)S(1)}, u32[]{:S(2)}, u32[]{:S(2)}) %collective-permute-start.27) | collective-permute-done | bytes 262176 | tf_op jit(solution)/shard_map/ppermute | solution.py:216
  128.5 1.5 %place.1 = bf16[32,16384]{1,0:T(8,128)(2,1)} custom-call(s32[4]{0:T(128)S(1)} %pad_add_fusion.at, bf16[32,4096]{1,0:T(8,128)(2,1)S(1)} %collective-permute-done.24.refs_0_, bf16[32,4096]{1,0:T(8,128)(2,1)S(1)} %collective-permute-done.25.refs_1_, bf16[32,4096]{1,0:T(8,128)(2,1)S(1)} %collective-permute-done.26.refs_2_, ...), custom_call_target="tpu_custom_call" | custom-call | bytes 2097152 | tf_op jit(solution)/shard_map/place/pallas_call | solution.py:193
  (62 shorter events, 13.6 us)
Async XLA Ops:
  0.0 13.6 %copy-start.1 = (f32[1,32,16384]{2,1,0:T(8,128)S(1)}, f32[1,32,16384]{2,1,0:T(8,128)}, u32[]{:S(2)}) copy-start(f32[1,32,16384]{2,1,0:T(8,128)} %param.9) | copy-start | bytes 6291460
  0.0 2.7 %copy-start.3 = (f32[4096]{0:T(1024)S(1)}, f32[4096]{0:T(1024)}, u32[]{:S(2)}) copy-start(f32[4096]{0:T(1024)} %param.12) | copy-start | bytes 49156
  0.0 2.7 %copy-start.4 = (f32[4096]{0:T(1024)S(1)}, f32[4096]{0:T(1024)}, u32[]{:S(2)}) copy-start(f32[4096]{0:T(1024)} %param.11) | copy-start | bytes 49156
  0.1 17.5 %copy-start.2 = (bf16[32,16384]{1,0:T(8,128)(2,1)S(1)}, bf16[32,16384]{1,0:T(8,128)(2,1)}, u32[]{:S(2)}) copy-start(bf16[32,16384]{1,0:T(8,128)(2,1)} %param.8) | copy-start | bytes 3145732
  2.3 11.3 %collective-permute-start = (bf16[64,4096]{1,0:T(8,128)(2,1)}, bf16[64,4096]{1,0:T(8,128)(2,1)}, u32[]{:S(2)}, u32[]{:S(2)}) collective-permute-start(bf16[64,4096]{1,0:T(8,128)(2,1)} %pad_maximum_fusion), channel_id=1, source_target_pairs={{0,8},{1,9},{2,10},{3,11},{4,12},{5,13},{6,14},{7,15},{8,0},{9,1},... | collective-permute-start | bytes 1572872 | tf_op jit(solution)/shard_map/ppermute | solution.py:216
  2.8 10.7 %collective-permute-start.18 = (f32[8704]{0:T(1024)S(1)}, f32[8704]{0:T(1024)S(1)}, u32[]{:S(2)}, u32[]{:S(2)}) collective-permute-start(f32[8704]{0:T(1024)S(1)} %pad_maximum_fusion.1), channel_id=1, source_target_pairs={{0,0},{1,8},{2,1},{3,9},{4,16},{5,24},{6,17},{7,25},{8,4},{9,12},{... | collective-permute-start | bytes 104456 | tf_op jit(solution)/shard_map/ppermute | solution.py:216
  10.2 31.8 %collective-permute-start.10 = (bf16[32,4096]{1,0:T(8,128)(2,1)}, bf16[32,4096]{1,0:T(8,128)(2,1)S(1)}, u32[]{:S(2)}, u32[]{:S(2)}) collective-permute-start(bf16[32,4096]{1,0:T(8,128)(2,1)} %convert_element_type.55), channel_id=1, source_target_pairs={{0,0},{1,8},{2,1},{3,9},{4,16},{5,24},{6,17},{7,25},{8,4},{9,12},{... | collective-permute-start | bytes 786440 | tf_op jit(solution)/shard_map/ppermute | solution.py:216
  13.5 12.2 %collective-permute-start.19 = (f32[512]{0:T(512)S(1)}, f32[512]{0:T(512)S(1)}, u32[]{:S(2)}, u32[]{:S(2)}) collective-permute-start(f32[512]{0:T(512)S(1)} %slice.22), channel_id=1, source_target_pairs={{0,8},{1,9},{2,10},{3,11},{4,12},{5,13},{6,14},{7,15},{8,0},{9,1},... | collective-permute-start | bytes 6152 | tf_op jit(solution)/shard_map/ppermute | solution.py:216
  15.3 22.9 %collective-permute-start.1 = (bf16[32,4096]{1,0:T(8,128)(2,1)}, bf16[32,4096]{1,0:T(8,128)(2,1)}, u32[]{:S(2)}, u32[]{:S(2)}) collective-permute-start(bf16[32,4096]{1,0:T(8,128)(2,1)} %fusion), channel_id=1, source_target_pairs={{0,16},{1,17},{2,18},{3,19},{4,20},{5,21},{6,22},{7,23},{8,24},{9,... | collective-permute-start | bytes 786440 | tf_op jit(solution)/shard_map/ppermute | solution.py:216
  18.6 26.3 %collective-permute-start.14 = (bf16[32,4096]{1,0:T(8,128)(2,1)}, bf16[32,4096]{1,0:T(8,128)(2,1)S(1)}, u32[]{:S(2)}, u32[]{:S(2)}) collective-permute-start(bf16[32,4096]{1,0:T(8,128)(2,1)} %get-tuple-element.17), channel_id=1, source_target_pairs={{0,0},{1,8},{2,1},{3,9},{4,16},{5,24},{6,17},{7,25},{8,4},{9,12},{... | collective-permute-start | bytes 786440 | tf_op jit(solution)/shard_map/ppermute | solution.py:216
  22.2 30.9 %collective-permute-start.15 = (bf16[32,4096]{1,0:T(8,128)(2,1)}, bf16[32,4096]{1,0:T(8,128)(2,1)S(1)}, u32[]{:S(2)}, u32[]{:S(2)}) collective-permute-start(bf16[32,4096]{1,0:T(8,128)(2,1)} %get-tuple-element.16), channel_id=1, source_target_pairs={{0,1},{1,9},{2,0},{3,8},{4,17},{5,25},{6,16},{7,24},{8,5},{9,13},{... | collective-permute-start | bytes 786440 | tf_op jit(solution)/shard_map/ppermute | solution.py:216
  25.7 29.3 %collective-permute-start.16 = (bf16[32,4096]{1,0:T(8,128)(2,1)}, bf16[32,4096]{1,0:T(8,128)(2,1)S(1)}, u32[]{:S(2)}, u32[]{:S(2)}) collective-permute-start(bf16[32,4096]{1,0:T(8,128)(2,1)} %get-tuple-element.18), channel_id=1, source_target_pairs={{0,16},{1,24},{2,17},{3,25},{4,0},{5,8},{6,1},{7,9},{8,20},{9,28},... | collective-permute-start | bytes 786440 | tf_op jit(solution)/shard_map/ppermute | solution.py:216
  38.2 16.9 %collective-permute-start.17 = (bf16[32,4096]{1,0:T(8,128)(2,1)}, bf16[32,4096]{1,0:T(8,128)(2,1)S(1)}, u32[]{:S(2)}, u32[]{:S(2)}) collective-permute-start(bf16[32,4096]{1,0:T(8,128)(2,1)} %get-tuple-element.15), channel_id=1, source_target_pairs={{0,17},{1,25},{2,16},{3,24},{4,1},{5,9},{6,0},{7,8},{8,21},{9,29},... | collective-permute-start | bytes 786440 | tf_op jit(solution)/shard_map/ppermute | solution.py:216
  41.9 13.7 %collective-permute-start.11 = (bf16[32,4096]{1,0:T(8,128)(2,1)S(1)}, bf16[32,4096]{1,0:T(8,128)(2,1)S(1)}, u32[]{:S(2)}, u32[]{:S(2)}) collective-permute-start(bf16[32,4096]{1,0:T(8,128)(2,1)S(1)} %collective-permute-done.10.refs_8_), channel_id=1, source_target_pairs={{0,1},{8,9},{1,0},{9,8},{16,17},{24,25},{17,16},{25,24},{4,5},{12,... | collective-permute-start | bytes 786440 | tf_op jit(solution)/shard_map/ppermute | solution.py:216
  44.9 19.6 %collective-permute-start.12 = (bf16[32,4096]{1,0:T(8,128)(2,1)S(1)}, bf16[32,4096]{1,0:T(8,128)(2,1)S(1)}, u32[]{:S(2)}, u32[]{:S(2)}) collective-permute-start(bf16[32,4096]{1,0:T(8,128)(2,1)S(1)} %collective-permute-done.10.refs_8_), channel_id=1, source_target_pairs={{0,16},{8,24},{1,17},{9,25},{16,0},{24,8},{17,1},{25,9},{4,20},{12... | collective-permute-start | bytes 786440 | tf_op jit(solution)/shard_map/ppermute | solution.py:216
  53.1 13.6 %collective-permute-start.2 = (bf16[32,4096]{1,0:T(8,128)(2,1)}, bf16[32,4096]{1,0:T(8,128)(2,1)S(1)}, u32[]{:S(2)}, u32[]{:S(2)}) collective-permute-start(bf16[32,4096]{1,0:T(8,128)(2,1)} %fusion.2), channel_id=1, source_target_pairs={{0,0},{1,8},{2,1},{3,9},{4,16},{5,24},{6,17},{7,25},{8,4},{9,12},{... | collective-permute-start | bytes 786440 | tf_op jit(solution)/shard_map/ppermute | solution.py:216
  55.0 12.3 %collective-permute-start.20 = (bf16[32,4096]{1,0:T(8,128)(2,1)S(1)}, bf16[32,4096]{1,0:T(8,128)(2,1)S(1)}, u32[]{:S(2)}, u32[]{:S(2)}) collective-permute-start(bf16[32,4096]{1,0:T(8,128)(2,1)S(1)} %collective-permute-done.14.refs_0_.refs_12_), channel_id=1, source_target_pairs={{0,8},{1,9},{2,10},{3,11},{4,12},{5,13},{6,14},{7,15},{8,0},{9,1},... | collective-permute-start | bytes 786440 | tf_op jit(solution)/shard_map/ppermute | solution.py:216
  55.1 13.9 %collective-permute-start.21 = (bf16[32,4096]{1,0:T(8,128)(2,1)S(1)}, bf16[32,4096]{1,0:T(8,128)(2,1)S(1)}, u32[]{:S(2)}, u32[]{:S(2)}) collective-permute-start(bf16[32,4096]{1,0:T(8,128)(2,1)S(1)} %collective-permute-done.15.refs_1_.refs_13_), channel_id=1, source_target_pairs={{0,8},{1,9},{2,10},{3,11},{4,12},{5,13},{6,14},{7,15},{8,0},{9,1},... | collective-permute-start | bytes 786440 | tf_op jit(solution)/shard_map/ppermute | solution.py:216
  55.7 15.2 %collective-permute-start.22 = (bf16[32,4096]{1,0:T(8,128)(2,1)S(1)}, bf16[32,4096]{1,0:T(8,128)(2,1)}, u32[]{:S(2)}, u32[]{:S(2)}) collective-permute-start(bf16[32,4096]{1,0:T(8,128)(2,1)S(1)} %collective-permute-done.16.refs_2_.refs_14_), channel_id=1, source_target_pairs={{0,8},{1,9},{2,10},{3,11},{4,12},{5,13},{6,14},{7,15},{8,0},{9,1},... | collective-permute-start | bytes 786440 | tf_op jit(solution)/shard_map/ppermute | solution.py:216
  64.4 7.7 %collective-permute-start.23 = (bf16[32,4096]{1,0:T(8,128)(2,1)S(1)}, bf16[32,4096]{1,0:T(8,128)(2,1)}, u32[]{:S(2)}, u32[]{:S(2)}) collective-permute-start(bf16[32,4096]{1,0:T(8,128)(2,1)S(1)} %collective-permute-done.17.refs_3_.refs_15_), channel_id=1, source_target_pairs={{0,8},{1,9},{2,10},{3,11},{4,12},{5,13},{6,14},{7,15},{8,0},{9,1},... | collective-permute-start | bytes 786440 | tf_op jit(solution)/shard_map/ppermute | solution.py:216
  66.7 7.6 %collective-permute-start.3 = (bf16[32,4096]{1,0:T(8,128)(2,1)S(1)}, bf16[32,4096]{1,0:T(8,128)(2,1)S(1)}, u32[]{:S(2)}, u32[]{:S(2)}) collective-permute-start(bf16[32,4096]{1,0:T(8,128)(2,1)S(1)} %collective-permute-done.2.refs_0_), channel_id=1, source_target_pairs={{0,1},{8,9},{1,0},{9,8},{16,17},{24,25},{17,16},{25,24},{4,5},{12,... | collective-permute-start | bytes 786440 | tf_op jit(solution)/shard_map/ppermute | solution.py:216
  67.3 8.1 %collective-permute-start.4 = (bf16[32,4096]{1,0:T(8,128)(2,1)S(1)}, bf16[32,4096]{1,0:T(8,128)(2,1)S(1)}, u32[]{:S(2)}, u32[]{:S(2)}) collective-permute-start(bf16[32,4096]{1,0:T(8,128)(2,1)S(1)} %collective-permute-done.2.refs_0_), channel_id=1, source_target_pairs={{0,16},{8,24},{1,17},{9,25},{16,0},{24,8},{17,1},{25,9},{4,20},{12... | collective-permute-start | bytes 786440 | tf_op jit(solution)/shard_map/ppermute | solution.py:216
  69.0 13.1 %collective-permute-start.5 = (bf16[32,4096]{1,0:T(8,128)(2,1)S(1)}, bf16[32,4096]{1,0:T(8,128)(2,1)S(1)}, u32[]{:S(2)}, u32[]{:S(2)}) collective-permute-start(bf16[32,4096]{1,0:T(8,128)(2,1)S(1)} %collective-permute-done.2.refs_0_), channel_id=1, source_target_pairs={{0,17},{8,25},{1,16},{9,24},{16,1},{24,9},{17,0},{25,8},{4,21},{12... | collective-permute-start | bytes 786440 | tf_op jit(solution)/shard_map/ppermute | solution.py:216
  70.8 20.8 %collective-permute-start.13 = (bf16[32,4096]{1,0:T(8,128)(2,1)S(1)}, bf16[32,4096]{1,0:T(8,128)(2,1)}, u32[]{:S(2)}, u32[]{:S(2)}) collective-permute-start(bf16[32,4096]{1,0:T(8,128)(2,1)S(1)} %collective-permute-done.10.refs_8_), channel_id=1, source_target_pairs={{0,17},{8,25},{1,16},{9,24},{16,1},{24,9},{17,0},{25,8},{4,21},{12... | collective-permute-start | bytes 786440 | tf_op jit(solution)/shard_map/ppermute | solution.py:216
  72.1 19.5 %collective-permute-start.6 = (bf16[32,4096]{1,0:T(8,128)(2,1)S(1)}, bf16[32,4096]{1,0:T(8,128)(2,1)}, u32[]{:S(2)}, u32[]{:S(2)}) collective-permute-start(bf16[32,4096]{1,0:T(8,128)(2,1)S(1)} %collective-permute-done.2.refs_0_), channel_id=1, source_target_pairs={{0,8},{1,9},{2,10},{3,11},{4,12},{5,13},{6,14},{7,15},{8,0},{9,1},... | collective-permute-start | bytes 786440 | tf_op jit(solution)/shard_map/ppermute | solution.py:216
  74.3 17.4 %collective-permute-start.7 = (bf16[32,4096]{1,0:T(8,128)(2,1)S(1)}, bf16[32,4096]{1,0:T(8,128)(2,1)}, u32[]{:S(2)}, u32[]{:S(2)}) collective-permute-start(bf16[32,4096]{1,0:T(8,128)(2,1)S(1)} %collective-permute-done.3.refs_1_), channel_id=1, source_target_pairs={{0,8},{1,9},{2,10},{3,11},{4,12},{5,13},{6,14},{7,15},{8,0},{9,1},... | collective-permute-start | bytes 786440 | tf_op jit(solution)/shard_map/ppermute | solution.py:216
  75.4 16.3 %collective-permute-start.8 = (bf16[32,4096]{1,0:T(8,128)(2,1)S(1)}, bf16[32,4096]{1,0:T(8,128)(2,1)}, u32[]{:S(2)}, u32[]{:S(2)}) collective-permute-start(bf16[32,4096]{1,0:T(8,128)(2,1)S(1)} %collective-permute-done.4.refs_2_), channel_id=1, source_target_pairs={{0,8},{1,9},{2,10},{3,11},{4,12},{5,13},{6,14},{7,15},{8,0},{9,1},... | collective-permute-start | bytes 786440 | tf_op jit(solution)/shard_map/ppermute | solution.py:216
  82.1 9.6 %collective-permute-start.9 = (bf16[32,4096]{1,0:T(8,128)(2,1)S(1)}, bf16[32,4096]{1,0:T(8,128)(2,1)}, u32[]{:S(2)}, u32[]{:S(2)}) collective-permute-start(bf16[32,4096]{1,0:T(8,128)(2,1)S(1)} %collective-permute-done.5.refs_3_), channel_id=1, source_target_pairs={{0,8},{1,9},{2,10},{3,11},{4,12},{5,13},{6,14},{7,15},{8,0},{9,1},... | collective-permute-start | bytes 786440 | tf_op jit(solution)/shard_map/ppermute | solution.py:216
  97.4 13.3 %collective-permute-start.24 = (bf16[32,4096]{1,0:T(8,128)(2,1)S(1)}, bf16[32,4096]{1,0:T(8,128)(2,1)S(1)}, u32[]{:S(2)}, u32[]{:S(2)}) collective-permute-start(bf16[32,4096]{1,0:T(8,128)(2,1)S(1)} %get-tuple-element.9), channel_id=1, source_target_pairs={{0,0},{8,1},{1,2},{9,3},{16,4},{24,5},{17,6},{25,7},{4,8},{12,9},{... | collective-permute-start | bytes 786440 | tf_op jit(solution)/shard_map/ppermute | solution.py:216
  100.8 13.4 %collective-permute-start.25 = (bf16[32,4096]{1,0:T(8,128)(2,1)S(1)}, bf16[32,4096]{1,0:T(8,128)(2,1)S(1)}, u32[]{:S(2)}, u32[]{:S(2)}) collective-permute-start(bf16[32,4096]{1,0:T(8,128)(2,1)S(1)} %get-tuple-element.10), channel_id=1, source_target_pairs={{1,0},{9,1},{0,2},{8,3},{17,4},{25,5},{16,6},{24,7},{5,8},{13,9},{... | collective-permute-start | bytes 786440 | tf_op jit(solution)/shard_map/ppermute | solution.py:216
  105.0 16.5 %collective-permute-start.26 = (bf16[32,4096]{1,0:T(8,128)(2,1)S(1)}, bf16[32,4096]{1,0:T(8,128)(2,1)S(1)}, u32[]{:S(2)}, u32[]{:S(2)}) collective-permute-start(bf16[32,4096]{1,0:T(8,128)(2,1)S(1)} %get-tuple-element.11), channel_id=1, source_target_pairs={{16,0},{24,1},{17,2},{25,3},{0,4},{8,5},{1,6},{9,7},{20,8},{28,9},... | collective-permute-start | bytes 786440 | tf_op jit(solution)/shard_map/ppermute | solution.py:216
  108.2 20.3 %collective-permute-start.27 = (bf16[32,4096]{1,0:T(8,128)(2,1)S(1)}, bf16[32,4096]{1,0:T(8,128)(2,1)S(1)}, u32[]{:S(2)}, u32[]{:S(2)}) collective-permute-start(bf16[32,4096]{1,0:T(8,128)(2,1)S(1)} %get-tuple-element.12), channel_id=1, source_target_pairs={{17,0},{25,1},{16,2},{24,3},{1,4},{9,5},{0,6},{8,7},{21,8},{29,9},... | collective-permute-start | bytes 786440 | tf_op jit(solution)/shard_map/ppermute | solution.py:216
  (4 other events, 9.6 us)
